TPU v7x, 128 devices: a whole 4x4x4 slice. The times are simulated.
128 devices in a mesh: rows: 64 (over z, y, x_hi, core), blk: 2 (over x_lo).
Axes of the slice: x: 4 (x_hi: 2, x_lo: 2; x = x_hi * 2 + x_lo), y: 4, z: 4, core: 2. Of those that a mesh axis runs over, the one named last changes fastest.
Arguments:
- text_emb: bfloat16 [16384, 4096], P('rows'), may hold values from -6 to 6
- quant_emb: bfloat16 [16384, 4096], P('rows'), may hold values from -6 to 6
- text_head: bfloat16 [4096, 2048], P(None, 'blk'), may hold values from -0.09375 to 0.09375
- quant_head: bfloat16 [4096, 2048], P(None, 'blk'), may hold values from -0.09375 to 0.09375
Outputs:
- grad_text: float32 [16384, 2048], P(('rows', 'blk'))
- grad_quant: float32 [16384, 2048], P(('rows', 'blk'))
All inputs are finite; a program needn't handle non-finite values.
Results may differ from a plain program's by a relative error of at most 0.0049.
Values may be sent and summed in bfloat16 or wider, within the bound.
A program may use at most 256 MiB of HBM per device.

v0:
```python
import jax
import jax.numpy as jnp
from jax import lax
from jax.sharding import PartitionSpec as P

ridge_weight = 0.05


def swapped(value, axis, distance):
    mask = 2**distance
    pairs = [(source, source ^ mask) for source in range(lax.axis_size(axis))]
    return lax.ppermute(value, axis, pairs)


def shards(text_emb, quant_emb, text_head, quant_head):
    device = lax.axis_index("blk")
    head_text = jnp.dot(text_emb, text_head, preferred_element_type=jnp.float32).astype(
        jnp.bfloat16
    )
    head_quant = jnp.dot(quant_emb, quant_head, preferred_element_type=jnp.float32).astype(
        jnp.bfloat16
    )
    full_text, full_quant = (
        lax.all_gather(head_text, "blk", axis=1, tiled=True),
        lax.all_gather(head_quant, "blk", axis=1, tiled=True),
    )
    rows_dev, width = full_text.shape
    total_rows = rows_dev * lax.axis_size("rows")
    contract = (((0,), (0,)), ((), ()))
    stacked = jnp.stack([full_text, full_quant], axis=0)
    own_feat = lax.dynamic_index_in_dim(stacked, device, 0, keepdims=False)
    partial_value = lax.dot_general(
        own_feat, own_feat, contract, preferred_element_type=jnp.float32
    )
    view_cov = lax.psum(partial_value, "rows")
    view_cov = view_cov / total_rows + ridge_weight * jnp.eye(width, dtype=jnp.float32)
    own_factor = jnp.linalg.cholesky(view_cov)
    own_white = jax.scipy.linalg.solve_triangular(
        own_factor, own_feat.astype(jnp.float32).T, lower=True
    )
    other_white = swapped(own_white, "blk", 0)
    own_grad = jax.scipy.linalg.solve_triangular(own_factor, other_white, lower=True, trans="T").T
    placed = lax.all_to_all(own_grad[None], "blk", split_axis=1, concat_axis=0, tiled=True)
    return (placed[0], placed[1])


def solution(mesh):
    placed = (P("rows", None), P("rows", None), P(None, "blk"), P(None, "blk"))
    return jax.shard_map(
        shards,
        mesh=mesh,
        in_specs=placed,
        out_specs=(P(("rows", "blk"), None), P(("rows", "blk"), None)),
        check_vma=False,
    )
```

profile of v0, /device:TPU:0, one launch (start us, length us, event | category | flops | bytes accessed | tf_op | source)
XLA Modules:
  0.0 1704.7 jit_solution(10789093360089796712)
XLA Ops:
  22.6 19.2 %all-gather.5.cloned.1.call-done = bf16[256,2048]{1,0:T(8,128)(2,1)} async-done(((bf16[256,1024]{1,0:T(8,128)(2,1)}), bf16[256,2048]{1,0:T(8,128)(2,1)}) %all-gather.5.cloned.1.call-update) | async-done | bytes 1048592 | tf_op jit(solution)/shard_map/all_gather | solution.py:25
  41.7 27.0 %all-gather.3.cloned.1.call-done = bf16[256,2048]{1,0:T(8,128)(2,1)} async-done(((bf16[256,1024]{1,0:T(8,128)(2,1)}), bf16[256,2048]{1,0:T(8,128)(2,1)}) %all-gather.3.cloned.1.call-update) | async-done | bytes 1048592 | tf_op jit(solution)/shard_map/all_gather | solution.py:24
  79.9 702.4 %all-reduce.3.cloned.1.call-done = f32[2048,2048]{0,1:T(8,128)} async-done(((f32[2048,2048]{0,1:T(8,128)}), f32[2048,2048]{0,1:T(8,128)}) %all-reduce.3.cloned.1.call-update) | async-done | bytes 16777232 | tf_op jit(solution)/shard_map/psum | solution.py:35
  782.3 12.4 select_add_fusion
  794.7 17.6 %copy.43 = f32[2048,2048]{1,0:T(8,128)} copy(f32[2048,2048]{0,1:T(8,128)} %select_add_fusion) | data formatting | bytes 33554432 | tf_op jit(solution)/shard_map/add | solution.py:36
  812.3 12.1 fusion
  830.1 11.7 cholesky.456
  842.0 9.8 custom-call.130
  857.4 11.7 cholesky.479
  869.2 10.0 custom-call.131
  892.5 11.7 cholesky.502
  905.1 10.2 custom-call.132
  923.4 11.7 cholesky.523
  935.9 9.9 custom-call.133
  954.9 11.7 cholesky.960
  967.4 10.0 custom-call.134
  979.1 8.1 fusion.29
  987.2 11.7 cholesky.980
  999.7 10.2 custom-call.135
  1011.5 8.7 fusion.26
  1020.2 11.7 cholesky.1000
  1032.7 9.9 custom-call.136
  1044.2 9.1 fusion.23
  1053.3 11.9 cholesky.1020
  1066.0 9.8 custom-call.137
  1077.3 9.1 fusion.41
  1086.4 12.1 cholesky.1040
  1099.3 9.8 custom-call.138
  1110.5 9.1 fusion.44
  1119.6 11.9 cholesky.1060
  1132.3 9.8 custom-call.139
  1143.4 8.6 fusion.47
  1152.1 11.9 cholesky.1080
  1164.8 9.8 custom-call.140
  1184.0 12.1 cholesky.1100
  1196.8 9.8 custom-call.141
  1215.0 11.9 cholesky.1120
  1227.6 9.8 custom-call.142
  1244.8 11.9 cholesky.1140
  1257.4 9.8 custom-call.143
  1273.1 11.7 cholesky.1160
  1285.5 9.8 custom-call.144
  1300.0 11.7 cholesky.1178
  1332.5 12.6 select_select_fusion
  1345.1 56.6 %while.1 = (s32[]{:T(128)}, f32[2048,2048]{0,1:T(8,128)}, s32[16,2]{0,1:T(2,128)S(1)}, f32[16,128,128]{2,1,0:T(8,128)}, s32[]{:T(128)}) while((s32[]{:T(128)}, f32[2048,2048]{0,1:T(8,128)}, s32[16,2]{0,1:T(2,128)S(1)}, f32[16,128,128]{2,1,0:T(8,128)}, s32[]{:T(128)}) %tuple.168), condition=%wide.while_cond, body=%wide.while_body.sunk | while | flops 2 | bytes 393329 | solution.py:42
  1401.7 158.8 %custom-call.145 = f32[16,128,128]{1,2,0:T(8,128)} custom-call(f32[16,128,128]{2,1,0:T(8,128)} %get-tuple-element.9), custom_call_target="InvertDiagBlocksLowerTriangular" | custom-call | tf_op jit(solution)/shard_map/jit(_solve_triangular)/triangular_solve | solution.py:42
  1603.0 44.7 %collective-permute-done = f32[2048,256]{1,0:T(8,128)S(1)} collective-permute-done((f32[2048,256]{1,0:T(8,128)S(1)}, f32[2048,256]{1,0:T(8,128)S(1)}, u32[]{:S(2)}, u32[]{:S(2)}) %collective-permute-start) | collective-permute-done | bytes 2097184 | tf_op jit(solution)/shard_map/ppermute | solution.py:12
  1670.5 24.6 %all_to_all.12 = f32[1,256,2048]{2,0,1:T(1,128)S(1)} all-to-all(f32[1,256,2048]{2,0,1:T(1,128)S(1)} %copy.76), channel_id=1, replica_groups=mesh['rows'=64,'blk'=2] {'blk'}, dimensions={1} | all-to-all | bytes 4194304 | tf_op jit(solution)/shard_map/all_to_all | solution.py:43
  (397 shorter events, 256.9 us)
Async XLA Ops:
  7.2 1.6 copy-start
  7.2 34.5 %all-gather.5.cloned.1.call-start = ((), (), s32[]{:S(2)}) async-start(), calls=%async_computation.2 | async-start | bytes 1572864 | tf_op jit(solution)/shard_map/all_gather | solution.py:25
  15.3 53.5 %all-gather.3.cloned.1.call-start = ((), (), s32[]{:S(2)}) async-start(), calls=%async_computation.1 | async-start | bytes 1572864 | tf_op jit(solution)/shard_map/all_gather | solution.py:24
  22.5 759.7 %all-reduce.3.cloned.1.call-start = ((), (), s32[]{:S(2)}) async-start(), calls=%async_computation.3 | async-start | bytes 33554432 | tf_op jit(solution)/shard_map/psum | solution.py:35
  824.4 5.7 copy-start.4
  879.2 2.1 copy-start.7
  882.4 5.7 copy-start.2
  1332.5 229.4 %copy-start.5 = (f32[2048,256]{0,1:T(8,128)S(1)}, f32[2048,256]{0,1:T(8,128)}, u32[]{:S(2)}) copy-start(f32[2048,256]{0,1:T(8,128)} %get-tuple-element.28) | copy-start | bytes 6291460
  1560.5 3.3 copy-start.6
  1560.5 16.3 copy-start.3
  1602.4 45.3 %collective-permute-start = (f32[2048,256]{1,0:T(8,128)S(1)}, f32[2048,256]{1,0:T(8,128)S(1)}, u32[]{:S(2)}, u32[]{:S(2)}) collective-permute-start(f32[2048,256]{1,0:T(8,128)S(1)} %convolution_dynamic-update-slice_fusion.13), channel_id=1, source_target_pairs={{0,1},{1,0},{2,3},{3,2},{4,5},{5,4},{6,7},{7,6},{8,9},{9,8},{10,11... | collective-permute-start | bytes 6291464 | tf_op jit(solution)/shard_map/ppermute | solution.py:12
  1664.4 1.4 copy-start.8
  1695.2 2.7 copy-start.1
Sparse Core Ops, SparseCore 0:
  15.4 26.2 all-gather.4
  44.0 24.7 all-gather.2
  80.0 702.2 all-reduce.2
where the time goes:
time: 1710 us; the launch traced here: 1700 us
  waiting for transfers between devices  793 us (46%)
  other arithmetic  547 us (32%)
  matrix products  202 us (12%)
  local copies, waits for them, and re-layouts  111 us (6%)
  between operations  26 us (2%)
  blocking collectives  24.6 us (1%)
    psum x1, waiting for transfers between devices, shards(): view_cov = lax.psum(partial_value, 'rows')  702 us
    another operation x62, other arithmetic, shards(): own_factor = jnp.linalg.cholesky(view_cov)  348 us
    another operation x3, other arithmetic, shards(): jax.scipy.linalg.solve_triangular(own_factor, other_white, lower=True, tr...  171 us
    another operation x30, matrix products, shards(): own_factor = jnp.linalg.cholesky(view_cov)  124 us
    another operation x80, local copies, waits for them, and re-layouts  56.4 us
    ppermute x1, waiting for transfers between devices, swapped(): return lax.ppermute(value, axis, pairs)  44.7 us
    another operation x31, matrix products, shards(): jax.scipy.linalg.solve_triangular(own_factor, own_feat.astype(jnp.float32...  41.6 us
  transfers between devices with their start and end apart: 4, of which 4 were waited for; matrix products, arithmetic and copies ran while one was open for 0% of the time, Pallas kernels for 0%

commit v1 on v0

v1 whole, which is shorter than its diff:
```python
import functools

import jax
import jax.numpy as jnp
from jax import lax
from jax.experimental import pallas as pl
from jax.experimental.pallas import tpu as pltpu
from jax.sharding import PartitionSpec as P

ridge_weight = 0.05
B = 256
NN = (((1,), (0,)), ((), ()))
NT = (((1,), (1,)), ((), ()))
TN = (((0,), (0,)), ((), ()))
MESH = pl.DeviceIdType.MESH
VMEM = pl.BlockSpec(memory_space=pltpu.VMEM)
HBM = pl.BlockSpec(memory_space=pl.ANY)


def mm(a, b, dims):
    return lax.dot_general(a, b, dims, preferred_element_type=jnp.float32)


def halves(x):
    hi = x.astype(jnp.bfloat16)
    return hi, (x - hi.astype(jnp.float32)).astype(jnp.bfloat16)


def dot3(a, b, dims):
    (ah, al), (bh, bl) = a, b
    return mm(ah, bh, dims) + (mm(ah, bl, dims) + mm(al, bh, dims))


def push(src, dst, send, recv, **device):
    return pltpu.make_async_remote_copy(
        src_ref=src, dst_ref=dst, send_sem=send, recv_sem=recv, device_id=device, device_id_type=MESH
    )

SEGMENTS = ((0, 4), (8, 8), (24, 4), (32, 2))


def inverse_factor(s_ref, a_ref, m_ref, bad_ref):
    rows = lax.broadcasted_iota(jnp.int32, (B, B), 0)
    cols = lax.broadcasted_iota(jnp.int32, (B, B), 1)
    eye = jnp.where(rows == cols, 1.0, 0.0)
    weight = jnp.where(rows > cols, 1.0, jnp.where(rows == cols, 0.5, 0.0))
    s = s_ref[...]
    on = jnp.where(rows == cols, s, 0.0)
    sc = lax.rsqrt(jnp.sum(on, axis=1, keepdims=True))
    sr = lax.rsqrt(jnp.sum(on, axis=0, keepdims=True))
    a = jnp.where(rows == cols, 1.0, s * sc * sr)
    step = eye - weight * (a - eye)
    m_ref[...] = step * sr
    a_ref[...] = a
    for turn in range(3):
        t = halves(eye - weight * (a_ref[...] - eye))
        if turn:
            m_ref[...] = dot3(t, halves(m_ref[...]), NN)
        a_ref[...] = dot3(halves(dot3(t, halves(a_ref[...]), NN)), t, NT)
    gap = a_ref[...] - eye
    bad_ref[...] += jnp.where(jnp.sum(gap * gap, axis=0, keepdims=True) <= 2.5e-5, 0.0, 1.0)
    m_ref[...] = dot3(halves(eye - weight * gap), halves(m_ref[...]), NN)


def step_kernel(
    total, ridge, h_ref, text_ref, quant_ref, flag_ref,
    feat, part, arrived, mine, cov, lh, ll, g, a_scr, m_scr, wh, wl, w_send, w_recv, gh, gl, num, back, returned, bad, bad2,
    e_send, e_recv, s_send, s_recv, x_send, x_recv, v_send, v_recv, u_send, u_recv, t_send, t_recv, w_s, w_r, b_s, b_r,
):
    at = lax.axis_index("rows")
    view = lax.axis_index("blk")
    core, xh, y, z = lax.rem(at, 2), lax.rem(at // 2, 2), lax.rem(at // 4, 4), at // 16
    twin = at + 1 - 2 * core
    half_cols = h_ref.shape[2]
    peers = arrived.shape[0]
    nb = lh.shape[0] // B
    per = half_cols // B
    starts = [sum(nb - c for c in range(k)) for k in range(nb)]
    order = [(i, j) for j in range(nb) for i in range(j, nb)]
    u, v = z + core * (y - z), y + core * (z - y)

    def device(p_u, p_v, p_x):
        pz, py = p_u + core * (p_v - p_u), p_v + core * (p_u - p_v)
        return ((pz * 4 + py) * 2 + p_x) * 2 + core

    def device_of(p):
        return device(p // 8, lax.rem(p // 2, 4), lax.rem(p, 2))

    me = (u * 4 + v) * 2 + xh

    barrier = pltpu.get_barrier_semaphore()

    def greet(d, _):
        pl.semaphore_signal(barrier, inc=1, device_id={"rows": device_of(lax.rem(me + d, peers))}, device_id_type=MESH)
        return 0

    lax.fori_loop(1, peers, greet, 0)
    pl.semaphore_signal(barrier, inc=1, device_id={"rows": twin}, device_id_type=MESH)
    pl.semaphore_signal(barrier, inc=1, device_id={"blk": 1 - view}, device_id_type=MESH)
    pl.semaphore_wait(barrier, peers + 1)

    swap = push(h_ref.at[1 - view], feat.at[core, view], e_send.at[0], e_recv.at[0], blk=1 - view)
    swap.start()
    first = push(h_ref.at[view], feat.at[core, view], e_send.at[1], e_recv.at[1], rows=twin)
    first.start()
    feat[core, view] = h_ref[view]
    swap.wait()
    second = push(feat.at[core, 1 - view], feat.at[core, 1 - view], e_send.at[2], e_recv.at[2], rows=twin)
    second.start()
    first.wait()
    second.wait()

    def cols(b):
        return lax.div(b, per), pl.ds(pl.multiple_of(lax.rem(b, per) * B, B), B)

    offset = 0
    spans = []
    for begin, count in SEGMENTS:
        rg = count * B // peers
        spans.append((begin, count, offset, rg))
        for t in range(count):
            (i0, j0), (i1, j1) = order[begin + t], order[begin + count + t]
            (hi, ci), (hj, cj) = cols(i0 + core * (i1 - i0)), cols(j0 + core * (j1 - j0))
            block = mm(feat[0, hi, :, ci], feat[0, hj, :, cj], TN) + mm(feat[1, hi, :, ci], feat[1, hj, :, cj], TN)
            n = B // rg
            part[t * n : (t + 1) * n, offset : offset + rg] = block.astype(jnp.bfloat16).reshape(n, rg, B)
        offset += rg

    def scatter(d):
        p = lax.rem(me + d, peers)
        return push(part.at[p], arrived.at[me], s_send.at[d], s_recv.at[d], rows=device_of(p))

    def landed(d):
        p = lax.rem(me + peers - d, peers)
        return push(part.at[p], arrived.at[p], s_send.at[d], s_recv.at[d], rows=device_of(p))

    lax.fori_loop(1, peers, lambda d, _: (scatter(d).start(), 0)[1], 0)
    mine[...] = part[me].astype(jnp.float32)

    def add(d, _):
        landed(d).wait_recv()
        mine[...] += arrived[lax.rem(me + peers - d, peers)].astype(jnp.float32)
        return 0

    lax.fori_loop(1, peers, add, 0)

    def rows_at(s, c, piece, count):
        begin, size, _, rg = spans[s]
        return pl.ds(pl.multiple_of((begin + c * size) * B + piece * rg, 16), count * rg)

    def same(rows, send, recv, dev):
        return push(cov.at[rows], cov.at[rows], send, recv, rows=dev)

    sent = []
    for s, (begin, size, off, rg) in enumerate(spans):
        cov[rows_at(s, core, me, 1)] = mine[off : off + rg] * (1.0 / total)
        copy = same(rows_at(s, core, me, 1), x_send.at[s], x_recv.at[s], device(u, v, 1 - xh))
        copy.start()
        sent.append(copy)
    other = me + 1 - 2 * xh
    for s in range(len(spans)):
        same(rows_at(s, core, other, 1), x_send.at[s], x_recv.at[s], at).wait_recv()

    def over_v(s, d, pv):
        return same(rows_at(s, core, (u * 4 + pv) * 2, 2), v_send.at[s, d], v_recv.at[s, d], device(u, lax.rem(v + d, 4), xh))

    def over_u(s, d, pu):
        return same(rows_at(s, core, pu * 8, 8), u_send.at[s, d], u_recv.at[s, d], device(lax.rem(u + d, 4), v, xh))

    def to_twin(s, d, c, pu):
        return same(rows_at(s, c, pu * 8, 8), t_send.at[s, d], t_recv.at[s, d], twin)

    for s in range(len(spans)):
        for d in range(1, 4):
            copy = over_v(s, d, v)
            copy.start()
            sent.append(copy)
    for s in range(len(spans)):
        for d in range(1, 4):
            over_v(s, d, lax.rem(v + 4 - d, 4)).wait_recv()
        for d in range(1, 4):
            copy = over_u(s, d, u)
            copy.start()
            sent.append(copy)
        copy = to_twin(s, 0, core, u)
        copy.start()
        sent.append(copy)

    def relay(s):
        for d in range(1, 4):
            pu = lax.rem(u + 4 - d, 4)
            over_u(s, d, pu).wait_recv()
            copy = to_twin(s, d, core, pu)
            copy.start()
            sent.append(copy)

    def ready(s):
        twin_u = y + core * (z - y)
        for d in range(4):
            to_twin(s, d, 1 - core, lax.rem(twin_u + 4 - d, 4)).wait_recv()

    rows = lax.broadcasted_iota(jnp.int32, (B, B), 0)
    lanes = lax.broadcasted_iota(jnp.int32, (B, B), 1)
    bad[...] = jnp.zeros_like(bad)
    relay(0)
    needs = {0: 0, 1: 1, 3: 2, 5: 3}
    for k in range(nb):
        if k in needs:
            ready(needs[k])
        kb, done = slice(k * B, (k + 1) * B), slice(0, k * B)

        def left(i, _):
            value = cov[pl.ds(pl.multiple_of((starts[k] - k + i) * B, B), B)]
            if k:
                ib = pl.ds(pl.multiple_of(i * B, B), B)
                value = value - dot3((lh[ib, done], ll[ib, done]), (lh[kb, done], ll[kb, done]), NT)
            g[i] = value
            return 0

        lax.fori_loop(k, nb, left, 0)
        g[k] = g[k] + jnp.where(rows == lanes, ridge, 0.0)
        inverse_factor(g.at[k], a_scr, m_scr, bad)
        mk = halves(m_scr[...])
        lh[kb, kb], ll[kb, kb] = mk
        if k < 3:
            relay(k + 1)

        def panel(i, _):
            ib = pl.ds(pl.multiple_of(i * B, B), B)
            lh[ib, kb], ll[ib, kb] = halves(dot3(halves(g[i]), (lh[kb, kb], ll[kb, kb]), NT))
            return 0

        if k < nb - 1:
            lax.fori_loop(k + 1, nb, panel, 0)
        f = feat[core, k // per, :, (k % per) * B : (k % per + 1) * B].astype(jnp.float32)
        if k:
            f = f - dot3((wh[:, done], wl[:, done]), (lh[kb, done], ll[kb, done]), NT)
        whi, wlo = halves(dot3(halves(f), mk, NT))
        w_send[k] = whi
        if k < nb - 1:
            wh[:, kb], wl[:, kb] = whi, wlo
        copy = push(w_send.at[k], w_recv.at[k], w_s.at[k], w_r.at[k], blk=1 - view)
        copy.start()
        sent.append(copy)
    flags = push(bad, bad2, w_s.at[nb], w_r.at[nb], blk=1 - view)
    flags.start()

    half = text_ref.shape[0]
    own = pl.ds(pl.multiple_of(view * half, half), half)
    away = pl.ds(pl.multiple_of((1 - view) * half, half), half)
    for k in reversed(range(nb)):
        kb, rest = slice(k * B, (k + 1) * B), slice((k + 1) * B, nb * B)
        push(w_send.at[k], w_recv.at[k], w_s.at[k], w_r.at[k], blk=1 - view).wait_recv()
        value = w_recv[k].astype(jnp.float32)
        if k < nb - 1:
            value = value - dot3((gh[:, rest], gl[:, rest]), (lh[rest, kb], ll[rest, kb]), NN)
        value = dot3(halves(value), (lh[kb, kb], ll[kb, kb]), NN)
        if k:
            gh[:, kb], gl[:, kb] = halves(value)
        num[...] = value
        back[k] = num[away].astype(jnp.bfloat16)
        copy = push(back.at[k], returned.at[k], b_s.at[k], b_r.at[k], blk=1 - view)
        copy.start()
        sent.append(copy)
        text_ref[:, kb] = num[own]
        quant_ref[:, kb] = num[own]
    for k in reversed(range(nb)):
        kb = slice(k * B, (k + 1) * B)
        push(back.at[k], returned.at[k], b_s.at[k], b_r.at[k], blk=1 - view).wait_recv()
        theirs = returned[k].astype(jnp.float32)

        @pl.when(view == 0)
        def _():
            quant_ref[:, kb] = theirs

        @pl.when(view == 1)
        def _():
            text_ref[:, kb] = theirs

    flags.wait()
    flag_ref[...] = bad[...] + bad2[...]
    for copy in sent:
        copy.wait_send()
    lax.fori_loop(1, peers, lambda d, _: (scatter(d).wait_send(), 0)[1], 0)


def whole_step(h, peers, total):
    _, rows, half = h.shape
    n = 2 * half
    nb = n // B
    blocks = nb * (nb + 1) // 4
    chunk = blocks * B // peers
    segs = len(SEGMENTS)
    dma = pltpu.SemaphoreType.DMA
    bf = jnp.bfloat16
    f32 = jnp.float32
    return pl.pallas_call(
        functools.partial(step_kernel, total, ridge_weight),
        out_shape=[jax.ShapeDtypeStruct((rows // 2, n), f32)] * 2 + [jax.ShapeDtypeStruct((8, B), f32)],
        in_specs=[VMEM],
        out_specs=[VMEM] * 3,
        scratch_shapes=[
            pltpu.VMEM((2, 2, rows, half), bf),
            pltpu.VMEM((peers, chunk, B), bf),
            pltpu.VMEM((peers, chunk, B), bf),
            pltpu.VMEM((chunk, B), f32),
            pltpu.VMEM((2 * blocks * B, B), f32),
            pltpu.VMEM((n, n), bf),
            pltpu.VMEM((n, n), bf),
            pltpu.VMEM((nb, B, B), f32),
            pltpu.VMEM((B, B), f32),
            pltpu.VMEM((B, B), f32),
            pltpu.VMEM((rows, n), bf),
            pltpu.VMEM((rows, n), bf),
            pltpu.VMEM((nb, rows, B), bf),
            pltpu.VMEM((nb, rows, B), bf),
            pltpu.VMEM((rows, n), bf),
            pltpu.VMEM((rows, n), bf),
            pltpu.VMEM((rows, B), f32),
            pltpu.VMEM((nb, rows // 2, B), bf),
            pltpu.VMEM((nb, rows // 2, B), bf),
            pltpu.VMEM((8, B), f32),
            pltpu.VMEM((8, B), f32),
            dma((3,)),
            dma((3,)),
            dma((peers,)),
            dma((peers,)),
            dma((segs,)),
            dma((segs,)),
            dma((segs, 4)),
            dma((segs, 4)),
            dma((segs, 4)),
            dma((segs, 4)),
            dma((segs, 4)),
            dma((segs, 4)),
            dma((nb + 1,)),
            dma((nb + 1,)),
            dma((nb,)),
            dma((nb,)),
        ],
        compiler_params=pltpu.CompilerParams(collective_id=0, has_side_effects=True, vmem_limit_bytes=60 << 20),
    )(h)


def direct_kernel(c_ref, m_ref, panel):
    nb = c_ref.shape[0] // B
    rows = lax.broadcasted_iota(jnp.int32, (B, B), 0)
    cols = lax.broadcasted_iota(jnp.int32, (B, B), 1)
    lane = lax.broadcasted_iota(jnp.int32, (1, B), 1)
    sub = lax.broadcasted_iota(jnp.int32, (B, 1), 0)

    def exact(a, b, dims):
        return lax.dot_general(a, b, dims, precision=lax.Precision.HIGHEST, preferred_element_type=jnp.float32)

    def at(i):
        return pl.ds(pl.multiple_of(i * B, B), B)

    def init(i, _):
        def column(j, _):
            m_ref[at(i), at(j)] = jnp.where(j > i, 0.0, c_ref[at(i), at(j)])
            return 0

        return lax.fori_loop(0, nb, column, 0)

    lax.fori_loop(0, nb, init, 0)

    def step(k, _):
        kb = at(k)
        panel[k] = m_ref[kb, kb]

        def pivot(j, _):
            s = panel[k]
            row = panel[k, pl.ds(j, 1), :]
            p = jnp.sum(jnp.where(lane == j, row, 0.0), axis=1, keepdims=True)
            col = jnp.sum(jnp.where(cols == j, s, 0.0), axis=1, keepdims=True)
            below = sub > j
            pivot_row = jnp.where(lane == j, 1.0, row)
            left = jnp.where(jnp.logical_and(cols == j, below), 0.0, s)
            panel[k] = left - jnp.where(below, col / p, 0.0) * pivot_row
            panel[k, pl.ds(j, 1), :] = jnp.where(lane <= j, pivot_row, 0.0) * lax.rsqrt(p)
            return 0

        lax.fori_loop(0, B, pivot, 0)
        m_ref[kb, kb] = panel[k]

        def inverse_row(j, _):
            m_ref[kb, at(j)] = exact(m_ref[kb, kb], m_ref[kb, at(j)], NN)
            return 0

        lax.fori_loop(0, k, inverse_row, 0)

        def factor(i, _):
            panel[i] = exact(m_ref[at(i), kb], m_ref[kb, kb], NT)
            m_ref[at(i), kb] = jnp.zeros((B, B), jnp.float32)
            return 0

        lax.fori_loop(k + 1, nb, factor, 0)

        def update(i, _):
            def inverse_part(j, _):
                m_ref[at(i), at(j)] = m_ref[at(i), at(j)] - exact(panel[i], m_ref[kb, at(j)], NN)
                return 0

            lax.fori_loop(0, k + 1, inverse_part, 0)

            def schur(j, _):
                m_ref[at(i), at(j)] = m_ref[at(i), at(j)] - exact(panel[i], panel[j], NT)
                return 0

            return lax.fori_loop(k + 1, i + 1, schur, 0)

        return lax.fori_loop(k + 1, nb, update, 0)

    lax.fori_loop(0, nb, step, 0)


def direct_step(h, total):
    view = lax.axis_index("blk")
    full = lax.all_gather(h, "blk", axis=2, tiled=True)
    feat = lax.dynamic_index_in_dim(full, view, 0, keepdims=False)
    n = feat.shape[1]
    cov = lax.psum(mm(feat, feat, TN), "rows") / total + ridge_weight * jnp.eye(n, dtype=jnp.float32)
    inverse = pl.pallas_call(
        direct_kernel,
        out_shape=jax.ShapeDtypeStruct((n, n), jnp.float32),
        in_specs=[VMEM],
        out_specs=VMEM,
        scratch_shapes=[pltpu.VMEM((n // B, B, B), jnp.float32)],
        compiler_params=pltpu.CompilerParams(vmem_limit_bytes=56 << 20),
    )(cov)
    exact = functools.partial(
        lax.dot_general, precision=lax.Precision.HIGHEST, preferred_element_type=jnp.float32
    )
    white = lax.ppermute(exact(feat.astype(jnp.float32), inverse, NT), "blk", [(0, 1), (1, 0)])
    grad = exact(white, inverse, NN)
    placed = lax.all_to_all(grad[None], "blk", split_axis=1, concat_axis=0, tiled=True)
    return placed[0], placed[1]


def shards(text_emb, quant_emb, text_head, quant_head):
    peers = lax.axis_size("rows") // 2
    total = text_emb.shape[0] * lax.axis_size("rows")
    h = jnp.stack(
        [
            jnp.dot(text_emb, text_head, preferred_element_type=jnp.float32).astype(jnp.bfloat16),
            jnp.dot(quant_emb, quant_head, preferred_element_type=jnp.float32).astype(jnp.bfloat16),
        ]
    )
    text, quant, flag = whole_step(h, peers, total)
    return lax.cond(jnp.max(flag) > 0, lambda: direct_step(h, total), lambda: (text, quant))


def solution(mesh):
    placed = (P("rows", None), P("rows", None), P(None, "blk"), P(None, "blk"))
    return jax.shard_map(
        shards,
        mesh=mesh,
        in_specs=placed,
        out_specs=(P(("rows", "blk"), None), P(("rows", "blk"), None)),
        check_vma=False,
    )
```

time: 1710 us -> 1420 us (0.83)
  other arithmetic: 547 us -> 13.9 us
  Pallas kernels: 0 us -> 524 us
  matrix products: 202 us -> 46.8 us
  local copies, waits for them, and re-layouts: 111 us -> 9.88 us
    pallas_call x0 -> x2, Pallas kernels: none -> 524 us  [the longest x1 358 us: direct_step(): pl.pallas_call(direct_kernel, out_shape=jax.ShapeDtypeStruct((n, n), jnp....]
    another operation x65 -> x1, other arithmetic: 519 us -> 0.1 us  [shards(): jnp.stack([jnp.dot(text_emb, text_head, preferred_element_type=jnp.float3...]
    another operation x92 -> x0, matrix products: 180 us -> none  [the longest x30 124 us: shards(): own_factor = jnp.linalg.cholesky(view_cov)]
    another operation x142 -> x0, local copies, waits for them, and re-layouts: 70.7 us -> none
    dot_general x1 -> x3, matrix products: 8.09 us -> 38.1 us  [the longest x1 14.8 us: direct_step(): grad = exact(white, inverse, NN)]
    add x1 -> x0, local copies, waits for them, and re-layouts: 17.6 us -> none  [shards(): view_cov / total_rows + ridge_weight * jnp.eye(width, dtype=jnp.float32)]
    all_gather x2 -> x1, waiting for transfers between devices: 46.2 us -> 30.8 us  [direct_step(): full = lax.all_gather(h, 'blk', axis=2, tiled=True)]
  transfers between devices with their start and end apart: 4 -> 3, of which waited for: 4 -> 3; matrix products, arithmetic and copies ran while one was open for 0% -> 0% of each run, Pallas kernels for 0% -> 0%
where the time goes in v1:
time: 1420 us; the launch traced here: 1410 us
  waiting for transfers between devices  778 us (55%)
  Pallas kernels  524 us (37%)
  matrix products  46.8 us (3%)
  blocking collectives  24.6 us (2%)
  between operations  15.3 us (1%)
    psum x1, waiting for transfers between devices, direct_step(): lax.psum(mm(feat, feat, TN), 'rows') / total  703 us
    pallas_call x1, Pallas kernels, direct_step(): pl.pallas_call(direct_kernel, out_shape=jax.ShapeDtypeStruct((n, n), jnp....  358 us
    pallas_call x1, Pallas kernels, whole_step(): pl.pallas_call(functools.partial(step_kernel, total, ridge_weight), out_s...  166 us
    ppermute x1, waiting for transfers between devices, direct_step(): lax.ppermute(exact(feat.astype(jnp.float32), inverse, NT), 'blk', [(0, 1)...  44.7 us
    all_gather x1, waiting for transfers between devices, direct_step(): full = lax.all_gather(h, 'blk', axis=2, tiled=True)  30.8 us
  transfers between devices with their start and end apart: 3, of which 3 were waited for; matrix products, arithmetic and copies ran while one was open for 0% of the time, Pallas kernels for 0%

profile of v1, /device:TPU:0, one launch (start us, length us, event | category | flops | bytes accessed | tf_op | source)
XLA Modules:
  0.0 1414.5 jit_solution(10536547177058515963)
XLA Ops:
  7.2 0.0 copy-start
  7.2 0.0 copy-start.5
  7.2 0.0 copy-start.6
  7.2 1.6 copy-done
  8.8 6.4 fusion.8
  15.2 0.0 copy-done.5
  15.2 0.0 copy-done.6
  15.2 2.4 fusion.9
  17.6 0.1 pad_maximum_fusion.h_ref
  17.7 166.0 %shard_map.63 = (f32[128,2048]{1,0:T(8,128)}, f32[128,2048]{1,0:T(8,128)S(1)}, f32[8,256]{1,0:T(8,128)}) custom-call(bf16[2,256,1024]{2,1,0:T(8,128)(2,1)S(1)} %pad_maximum_fusion.h_ref), custom_call_target="tpu_custom_call" | custom-call | tf_op jit(solution)/shard_map/pallas_call | solution.py:297
  183.7 1.3 reduce_max.9
  185.7 1218.0 %conditional.1 = ((f32[128,2048]{1,0:T(8,128)}, f32[128,2048]{1,0:T(8,128)S(1)})) conditional(s32[]{:T(128)} %convert_element_type.13, (f32[128,2048]{1,0:T(8,128)}, f32[128,2048]{1,0:T(8,128)S(1)}) %tuple.14, bf16[2,256,1024]{2,1,0:T(8,128)(2,1)S(1)} %pad_maximum_fusion.h_ref), branch_computations={%region_1.0_spmd, %region_2.4_spmd} | conditional | flops 27938258944 | bytes 307233024 | solution.py:450
  185.7 0.0 copy-start.3
  185.7 0.0 all-gather.2.cloned.1.call-start
  185.7 0.9 copy-done.3
  186.7 0.0 all-gather.2.cloned.1.call-update
  186.7 0.3 all-reduce.2.cloned.1.call-start
  187.0 30.8 %all-gather.2.cloned.1.call-done = bf16[2,256,2048]{2,1,0:T(8,128)(2,1)} async-done(((bf16[2,256,1024]{2,1,0:T(8,128)(2,1)}), bf16[2,256,2048]{2,1,0:T(8,128)(2,1)}) %all-gather.2.cloned.1.call-update) | async-done | bytes 2097168 | tf_op jit(solution)/shard_map/cond/branch_1_fun/all_gather | solution.py:419
  217.8 9.6 fusion.2
  227.4 0.0 all-reduce.2.cloned.1.call-update
  227.4 702.6 %all-reduce.2.cloned.1.call-done = f32[2048,2048]{1,0:T(8,128)} async-done(((f32[2048,2048]{1,0:T(8,128)}), f32[2048,2048]{1,0:T(8,128)}) %all-reduce.2.cloned.1.call-update) | async-done | bytes 16777232 | tf_op jit(solution)/shard_map/cond/branch_1_fun/psum | solution.py:422
  930.0 12.5 select_add_fusion.c_ref
  942.5 0.0 copy-start.4
  942.5 358.2 %branch_1_fun.1 = f32[2048,2048]{1,0:T(8,128)} custom-call(f32[2048,2048]{1,0:T(8,128)} %select_add_fusion.c_ref), custom_call_target="tpu_custom_call" | custom-call | tf_op jit(solution)/shard_map/cond/branch_1_fun/pallas_call | solution.py:423
  1300.7 0.0 copy-done.4
  1300.7 0.0 copy-start.2
  1300.7 13.6 fusion
  1314.3 0.9 collective-permute-start
  1315.3 44.7 %collective-permute-done = f32[256,2048]{1,0:T(8,128)S(1)} collective-permute-done((f32[256,2048]{1,0:T(8,128)S(1)}, f32[256,2048]{1,0:T(8,128)S(1)}, u32[]{:S(2)}, u32[]{:S(2)}) %collective-permute-start) | collective-permute-done | bytes 2097184 | tf_op jit(solution)/shard_map/cond/branch_1_fun/ppermute | solution.py:434
  1359.9 0.0 copy-done.2
  1359.9 14.8 %convolution_bitcast_fusion = f32[1,256,2048]{2,1,0:T(8,128)S(1)} fusion(f32[256,2048]{1,0:T(8,128)S(1)} %collective-permute-done, f32[2048,2048]{1,0:T(8,128)S(1)} %copy-done.2), kind=kOutput, calls=%fused_computation.2 | convolution fusion | flops 12884901888 | bytes 20971520 | tf_op jit(solution)/shard_map/cond/branch_1_fun/dot_general | solution.py:435
  1374.7 2.2 copy.10
  1376.9 24.6 %all_to_all.10 = f32[1,256,2048]{2,0,1:T(1,128)S(1)} all-to-all(f32[1,256,2048]{2,0,1:T(1,128)S(1)} %copy.10), channel_id=1, replica_groups=mesh['rows'=64,'blk'=2] {'blk'}, dimensions={1} | all-to-all | bytes 4194304 | tf_op jit(solution)/shard_map/cond/branch_1_fun/all_to_all | solution.py:436
  1401.5 0.1 slice.8
  1401.6 1.3 copy.16
  1402.9 0.1 slice.9
  1402.9 0.3 copy.17
  1403.6 0.0 copy-start.1
  1403.6 2.4 copy.25
  1406.1 1.0 copy.26
  1407.1 0.0 copy-done.1
Async XLA Ops:
  7.2 1.6 copy-start
  7.2 8.0 copy-start.5
  7.2 8.0 copy-start.6
  185.7 1.0 copy-start.3
  185.7 32.1 %all-gather.2.cloned.1.call-start = ((), (), s32[]{:S(2)}) async-start(), calls=%async_computation.1 | async-start | bytes 3145728 | tf_op jit(solution)/shard_map/cond/branch_1_fun/all_gather | solution.py:419
  186.7 743.4 %all-reduce.2.cloned.1.call-start = ((), (), s32[]{:S(2)}) async-start(), calls=%async_computation.2 | async-start | bytes 33554432 | tf_op jit(solution)/shard_map/cond/branch_1_fun/psum | solution.py:422
  942.5 358.2 %copy-start.4 = (bf16[2,256,2048]{2,1,0:T(8,128)(2,1)S(1)}, bf16[2,256,2048]{2,1,0:T(8,128)(2,1)}, u32[]{:S(2)}) copy-start(bf16[2,256,2048]{2,1,0:T(8,128)(2,1)} %all-gather.2.cloned.1.call-done) | copy-start | bytes 6291460 | tf_op jit(solution)/shard_map/cond
  1300.7 59.2 %copy-start.2 = (f32[2048,2048]{1,0:T(8,128)S(1)}, f32[2048,2048]{1,0:T(8,128)}, u32[]{:S(2)}) copy-start(f32[2048,2048]{1,0:T(8,128)} %branch_1_fun.1) | copy-start | bytes 50331652 | tf_op jit(solution)/shard_map/cond
  1314.3 45.6 %collective-permute-start = (f32[256,2048]{1,0:T(8,128)S(1)}, f32[256,2048]{1,0:T(8,128)S(1)}, u32[]{:S(2)}, u32[]{:S(2)}) collective-permute-start(f32[256,2048]{1,0:T(8,128)S(1)} %fusion), channel_id=1, source_target_pairs={{0,1},{1,0},{2,3},{3,2},{4,5},{5,4},{6,7},{7,6},{8,9},{9,8},{10,11... | collective-permute-start | bytes 6291464 | tf_op jit(solution)/shard_map/cond/branch_1_fun/ppermute | solution.py:434
  1403.6 3.4 copy-start.1
Sparse Core Ops, SparseCore 0:
  188.8 28.9 all-gather.1
  227.6 702.4 all-reduce.1

commit v2 on v1

--- a/solution.py
+++ b/solution.py
@@ -36,7 +36,8 @@
         src_ref=src, dst_ref=dst, send_sem=send, recv_sem=recv, device_id=device, device_id_type=MESH
     )
 
-SEGMENTS = ((0, 4), (8, 8), (24, 4), (32, 2))
+SEGMENTS = ((0, 4), (8, 4), (16, 4), (24, 4), (32, 2))
+EARLY = 2
 
 
 def inverse_factor(s_ref, a_ref, m_ref, bad_ref):
@@ -126,23 +127,32 @@
             part[t * n : (t + 1) * n, offset : offset + rg] = block.astype(jnp.bfloat16).reshape(n, rg, B)
         offset += rg
 
-    def scatter(d):
+    cut = spans[EARLY][2]
+    waves = [(0, cut), (cut, mine.shape[0] - cut)]
+
+    def scatter(w, d):
         p = lax.rem(me + d, peers)
-        return push(part.at[p], arrived.at[me], s_send.at[d], s_recv.at[d], rows=device_of(p))
-
-    def landed(d):
+        piece = pl.ds(*waves[w])
+        return push(part.at[p, piece], arrived.at[me, piece], s_send.at[w, d], s_recv.at[w, d], rows=device_of(p))
+
+    def landed(w, d):
         p = lax.rem(me + peers - d, peers)
-        return push(part.at[p], arrived.at[p], s_send.at[d], s_recv.at[d], rows=device_of(p))
-
-    lax.fori_loop(1, peers, lambda d, _: (scatter(d).start(), 0)[1], 0)
-    mine[...] = part[me].astype(jnp.float32)
-
-    def add(d, _):
-        landed(d).wait_recv()
-        mine[...] += arrived[lax.rem(me + peers - d, peers)].astype(jnp.float32)
-        return 0
-
-    lax.fori_loop(1, peers, add, 0)
+        piece = pl.ds(*waves[w])
+        return push(part.at[p, piece], arrived.at[p, piece], s_send.at[w, d], s_recv.at[w, d], rows=device_of(p))
+
+    for w in range(2):
+        lax.fori_loop(1, peers, lambda d, _: (scatter(w, d).start(), 0)[1], 0)
+
+    def reduce(w):
+        piece = pl.ds(*waves[w])
+        mine[piece] = part[me, piece].astype(jnp.float32)
+
+        def add(d, _):
+            landed(w, d).wait_recv()
+            mine[piece] += arrived[lax.rem(me + peers - d, peers), piece].astype(jnp.float32)
+            return 0
+
+        lax.fori_loop(1, peers, add, 0)
 
     def rows_at(s, c, piece, count):
         begin, size, _, rg = spans[s]
@@ -152,14 +162,13 @@
         return push(cov.at[rows], cov.at[rows], send, recv, rows=dev)
 
     sent = []
-    for s, (begin, size, off, rg) in enumerate(spans):
-        cov[rows_at(s, core, me, 1)] = mine[off : off + rg] * (1.0 / total)
-        copy = same(rows_at(s, core, me, 1), x_send.at[s], x_recv.at[s], device(u, v, 1 - xh))
+
+    def go(copy):
         copy.start()
         sent.append(copy)
-    other = me + 1 - 2 * xh
-    for s in range(len(spans)):
-        same(rows_at(s, core, other, 1), x_send.at[s], x_recv.at[s], at).wait_recv()
+
+    def over_x(s, piece):
+        return same(rows_at(s, core, piece, 1), x_send.at[s], x_recv.at[s], device(u, v, 1 - xh))
 
     def over_v(s, d, pv):
         return same(rows_at(s, core, (u * 4 + pv) * 2, 2), v_send.at[s, d], v_recv.at[s, d], device(u, lax.rem(v + d, 4), xh))
@@ -170,29 +179,31 @@
     def to_twin(s, d, c, pu):
         return same(rows_at(s, c, pu * 8, 8), t_send.at[s, d], t_recv.at[s, d], twin)
 
-    for s in range(len(spans)):
-        for d in range(1, 4):
-            copy = over_v(s, d, v)
-            copy.start()
-            sent.append(copy)
-    for s in range(len(spans)):
-        for d in range(1, 4):
-            over_v(s, d, lax.rem(v + 4 - d, 4)).wait_recv()
-        for d in range(1, 4):
-            copy = over_u(s, d, u)
-            copy.start()
-            sent.append(copy)
-        copy = to_twin(s, 0, core, u)
-        copy.start()
-        sent.append(copy)
+    def near(segments):
+        for s in segments:
+            _, _, off, rg = spans[s]
+            cov[rows_at(s, core, me, 1)] = mine[off : off + rg] * (1.0 / total)
+            go(over_x(s, me))
+
+    def middle(segments):
+        for s in segments:
+            over_x(s, me + 1 - 2 * xh).wait_recv()
+            for d in range(1, 4):
+                go(over_v(s, d, v))
+
+    def far(segments):
+        for s in segments:
+            for d in range(1, 4):
+                over_v(s, d, lax.rem(v + 4 - d, 4)).wait_recv()
+            for d in range(1, 4):
+                go(over_u(s, d, u))
+            go(to_twin(s, 0, core, u))
 
     def relay(s):
         for d in range(1, 4):
             pu = lax.rem(u + 4 - d, 4)
             over_u(s, d, pu).wait_recv()
-            copy = to_twin(s, d, core, pu)
-            copy.start()
-            sent.append(copy)
+            go(to_twin(s, d, core, pu))
 
     def ready(s):
         twin_u = y + core * (z - y)
@@ -202,8 +213,17 @@
     rows = lax.broadcasted_iota(jnp.int32, (B, B), 0)
     lanes = lax.broadcasted_iota(jnp.int32, (B, B), 1)
     bad[...] = jnp.zeros_like(bad)
+    early, late = range(EARLY), range(EARLY, len(spans))
+    reduce(0)
+    near(early)
+    middle(early)
+    far(early)
+    reduce(1)
+    near(late)
+    middle(late)
     relay(0)
-    needs = {0: 0, 1: 1, 3: 2, 5: 3}
+    far(late)
+    needs = {0: 0, 1: 1, 2: 2, 3: 3, 5: 4}
     for k in range(nb):
         if k in needs:
             ready(needs[k])
@@ -222,7 +242,7 @@
         inverse_factor(g.at[k], a_scr, m_scr, bad)
         mk = halves(m_scr[...])
         lh[kb, kb], ll[kb, kb] = mk
-        if k < 3:
+        if k + 1 < len(spans):
             relay(k + 1)
 
         def panel(i, _):
@@ -239,9 +259,7 @@
         w_send[k] = whi
         if k < nb - 1:
             wh[:, kb], wl[:, kb] = whi, wlo
-        copy = push(w_send.at[k], w_recv.at[k], w_s.at[k], w_r.at[k], blk=1 - view)
-        copy.start()
-        sent.append(copy)
+        go(push(w_send.at[k], w_recv.at[k], w_s.at[k], w_r.at[k], blk=1 - view))
     flags = push(bad, bad2, w_s.at[nb], w_r.at[nb], blk=1 - view)
     flags.start()
 
@@ -259,9 +277,7 @@
             gh[:, kb], gl[:, kb] = halves(value)
         num[...] = value
         back[k] = num[away].astype(jnp.bfloat16)
-        copy = push(back.at[k], returned.at[k], b_s.at[k], b_r.at[k], blk=1 - view)
-        copy.start()
-        sent.append(copy)
+        go(push(back.at[k], returned.at[k], b_s.at[k], b_r.at[k], blk=1 - view))
         text_ref[:, kb] = num[own]
         quant_ref[:, kb] = num[own]
     for k in reversed(range(nb)):
@@ -278,10 +294,11 @@
             text_ref[:, kb] = theirs
 
     flags.wait()
-    flag_ref[...] = bad[...] + bad2[...]
+    flag_ref[0] = jnp.sum(bad[...] + bad2[...])
     for copy in sent:
         copy.wait_send()
-    lax.fori_loop(1, peers, lambda d, _: (scatter(d).wait_send(), 0)[1], 0)
+    for w in range(2):
+        lax.fori_loop(1, peers, lambda d, _: (scatter(w, d).wait_send(), 0)[1], 0)
 
 
 def whole_step(h, peers, total):
@@ -296,9 +313,9 @@
     f32 = jnp.float32
     return pl.pallas_call(
         functools.partial(step_kernel, total, ridge_weight),
-        out_shape=[jax.ShapeDtypeStruct((rows // 2, n), f32)] * 2 + [jax.ShapeDtypeStruct((8, B), f32)],
+        out_shape=[jax.ShapeDtypeStruct((rows // 2, n), f32)] * 2 + [jax.ShapeDtypeStruct((1,), f32)],
         in_specs=[VMEM],
-        out_specs=[VMEM] * 3,
+        out_specs=[VMEM] * 2 + [pl.BlockSpec(memory_space=pltpu.SMEM)],
         scratch_shapes=[
             pltpu.VMEM((2, 2, rows, half), bf),
             pltpu.VMEM((peers, chunk, B), bf),
@@ -323,8 +340,8 @@
             pltpu.VMEM((8, B), f32),
             dma((3,)),
             dma((3,)),
-            dma((peers,)),
-            dma((peers,)),
+            dma((2, peers)),
+            dma((2, peers)),
             dma((segs,)),
             dma((segs,)),
             dma((segs, 4)),
@@ -416,10 +433,21 @@
 
 def direct_step(h, total):
     view = lax.axis_index("blk")
-    full = lax.all_gather(h, "blk", axis=2, tiled=True)
-    feat = lax.dynamic_index_in_dim(full, view, 0, keepdims=False)
+    ranks = lax.axis_size("rows")
+
+    def swapped(x):
+        return lax.ppermute(x, "blk", [(0, 1), (1, 0)])
+
+    near = lax.dynamic_index_in_dim(h, view, 0, keepdims=False)
+    far = swapped(lax.dynamic_index_in_dim(h, 1 - view, 0, keepdims=False))
+    feat = jnp.where(view == 0, jnp.concatenate([near, far], 1), jnp.concatenate([far, near], 1))
     n = feat.shape[1]
-    cov = lax.psum(mm(feat, feat, TN), "rows") / total + ridge_weight * jnp.eye(n, dtype=jnp.float32)
+    cov = mm(feat, feat, TN)
+    hop = 1
+    while hop < ranks:
+        cov = cov + lax.ppermute(cov, "rows", [(r, r ^ hop) for r in range(ranks)])
+        hop *= 2
+    cov = cov / total + ridge_weight * jnp.eye(n, dtype=jnp.float32)
     inverse = pl.pallas_call(
         direct_kernel,
         out_shape=jax.ShapeDtypeStruct((n, n), jnp.float32),
@@ -431,10 +459,12 @@
     exact = functools.partial(
         lax.dot_general, precision=lax.Precision.HIGHEST, preferred_element_type=jnp.float32
     )
-    white = lax.ppermute(exact(feat.astype(jnp.float32), inverse, NT), "blk", [(0, 1), (1, 0)])
+    white = swapped(exact(feat.astype(jnp.float32), inverse, NT))
     grad = exact(white, inverse, NN)
-    placed = lax.all_to_all(grad[None], "blk", split_axis=1, concat_axis=0, tiled=True)
-    return placed[0], placed[1]
+    half = grad.shape[0] // 2
+    own = lax.dynamic_slice_in_dim(grad, view * half, half, 0)
+    other = swapped(lax.dynamic_slice_in_dim(grad, (1 - view) * half, half, 0))
+    return jnp.where(view == 0, own, other), jnp.where(view == 0, other, own)
 
 
 def shards(text_emb, quant_emb, text_head, quant_head):
@@ -447,7 +477,7 @@
         ]
     )
     text, quant, flag = whole_step(h, peers, total)
-    return lax.cond(jnp.max(flag) > 0, lambda: direct_step(h, total), lambda: (text, quant))
+    return lax.cond(flag[0] > 0, lambda: direct_step(h, total), lambda: (text, quant))
 
 
 def solution(mesh):

time: 1420 us -> 2550 us (1.80)
  waiting for transfers between devices: 778 us -> 1900 us
  other arithmetic: 13.9 us -> 73.9 us
    ppermute x1 -> x9, waiting for transfers between devices: 44.7 us -> 1900 us  [the longest x6 1830 us: direct_step(): cov = cov + lax.ppermute(cov, 'rows', [(r, r ^ hop) for r in range(ranks)])]
    psum x1 -> x0, waiting for transfers between devices: 703 us -> none  [direct_step(): lax.psum(mm(feat, feat, TN), 'rows') / total]
    add x1 -> x6, other arithmetic: 12.5 us -> 72.3 us  [the longest x5 59.7 us: direct_step(): cov = cov + lax.ppermute(cov, 'rows', [(r, r ^ hop) for r in range(ranks)])]
    all_gather x1 -> x0, waiting for transfers between devices: 30.8 us -> none  [direct_step(): full = lax.all_gather(h, 'blk', axis=2, tiled=True)]
  transfers between devices with their start and end apart: 3 -> 9, of which waited for: 3 -> 9; matrix products, arithmetic and copies ran while one was open for 0% -> 0% of each run, Pallas kernels for 0% -> 0%
where the time goes in v2:
time: 2550 us; the launch traced here: 2540 us
  waiting for transfers between devices  1900 us (75%)
  Pallas kernels  507 us (20%)
  other arithmetic  73.9 us (3%)
  matrix products  42.2 us (2%)
    ppermute x6, waiting for transfers between devices, direct_step(): cov = cov + lax.ppermute(cov, 'rows', [(r, r ^ hop) for r in range(ranks)])  1830 us
    pallas_call x1, Pallas kernels, direct_step(): pl.pallas_call(direct_kernel, out_shape=jax.ShapeDtypeStruct((n, n), jnp....  358 us
    pallas_call x1, Pallas kernels, whole_step(): pl.pallas_call(functools.partial(step_kernel, total, ridge_weight), out_s...  149 us
    ppermute x3, waiting for transfers between devices, swapped(): return lax.ppermute(x, 'blk', [(0, 1), (1, 0)])  75.6 us
    add x5, other arithmetic, direct_step(): cov = cov + lax.ppermute(cov, 'rows', [(r, r ^ hop) for r in range(ranks)])  59.7 us
  transfers between devices with their start and end apart: 9, of which 9 were waited for; matrix products, arithmetic and copies ran while one was open for 0% of the time, Pallas kernels for 0%

profile of v2, /device:TPU:0, one launch (start us, length us, event | category | flops | bytes accessed | tf_op | source)
XLA Modules:
  0.0 2543.8 jit_solution(3841771322773133598)
XLA Ops:
  0.6 0.0 copy-start
  0.6 0.0 copy-start.2
  0.7 0.0 copy-start.3
  0.7 1.6 copy-done
  2.2 6.4 fusion.4
  8.6 0.0 copy-done.2
  8.6 0.0 copy-done.3
  8.6 2.4 fusion.5
  11.0 0.1 pad_maximum_fusion.h_ref
  11.1 148.7 %shard_map.63 = (f32[128,2048]{1,0:T(8,128)}, f32[128,2048]{1,0:T(8,128)}, f32[1]{0:T(128)}) custom-call(bf16[2,256,1024]{2,1,0:T(8,128)(2,1)S(1)} %pad_maximum_fusion.h_ref), custom_call_target="tpu_custom_call" | custom-call | tf_op jit(solution)/shard_map/pallas_call | solution.py:314
  160.4 2378.5 %conditional.1 = ((f32[128,2048]{1,0:T(8,128)}, f32[128,2048]{1,0:T(8,128)})) conditional(s32[]{:T(128)} %bitcast.4, (f32[128,2048]{1,0:T(8,128)}, f32[128,2048]{1,0:T(8,128)}) %tuple.14, bf16[2,256,1024]{2,1,0:T(8,128)(2,1)S(1)} %pad_maximum_fusion.h_ref), branch_computations={%region_0.0_spmd, %region_1.2_spmd} | conditional | flops 27969191936 | bytes 786432384 | solution.py:480
  160.4 0.1 dynamic-slice_bitcast_fusion.1
  160.5 1.1 collective-permute-start
  161.6 12.4 collective-permute-done
  174.0 2.4 fusion.1
  176.4 0.1 collective-permute-start.1
  176.5 25.3 collective-permute-done.1
  201.8 12.1 add.26
  213.9 1.5 collective-permute-start.2
  215.4 362.6 %collective-permute-done.2 = f32[2048,2048]{1,0:T(8,128)} collective-permute-done((f32[2048,2048]{1,0:T(8,128)}, f32[2048,2048]{1,0:T(8,128)}, u32[]{:S(2)}, u32[]{:S(2)}) %collective-permute-start.2) | collective-permute-done | bytes 16777248 | tf_op jit(solution)/shard_map/cond/branch_1_fun/ppermute | solution.py:448
  578.0 11.6 add.27
  589.6 0.4 collective-permute-start.3
  590.1 361.2 %collective-permute-done.3 = f32[2048,2048]{1,0:T(8,128)} collective-permute-done((f32[2048,2048]{1,0:T(8,128)S(1)}, f32[2048,2048]{1,0:T(8,128)}, u32[]{:S(2)}, u32[]{:S(2)}) %collective-permute-start.3) | collective-permute-done | bytes 16777248 | tf_op jit(solution)/shard_map/cond/branch_1_fun/ppermute | solution.py:448
  951.3 12.1 add.28
  963.4 2.3 collective-permute-start.4
  965.7 360.0 %collective-permute-done.4 = f32[2048,2048]{1,0:T(8,128)} collective-permute-done((f32[2048,2048]{1,0:T(8,128)}, f32[2048,2048]{1,0:T(8,128)}, u32[]{:S(2)}, u32[]{:S(2)}) %collective-permute-start.4) | collective-permute-done | bytes 16777248 | tf_op jit(solution)/shard_map/cond/branch_1_fun/ppermute | solution.py:448
  1325.7 11.6 add.29
  1337.4 2.1 collective-permute-start.5
  1339.5 358.0 %collective-permute-done.5 = f32[2048,2048]{1,0:T(8,128)} collective-permute-done((f32[2048,2048]{1,0:T(8,128)S(1)}, f32[2048,2048]{1,0:T(8,128)}, u32[]{:S(2)}, u32[]{:S(2)}) %collective-permute-start.5) | collective-permute-done | bytes 16777248 | tf_op jit(solution)/shard_map/cond/branch_1_fun/ppermute | solution.py:448
  1697.4 12.1 add.30
  1709.6 0.6 collective-permute-start.6
  1710.1 360.2 %collective-permute-done.6 = f32[2048,2048]{1,0:T(8,128)S(1)} collective-permute-done((f32[2048,2048]{1,0:T(8,128)}, f32[2048,2048]{1,0:T(8,128)S(1)}, u32[]{:S(2)}, u32[]{:S(2)}) %collective-permute-start.6) | collective-permute-done | bytes 16777248 | tf_op jit(solution)/shard_map/cond/branch_1_fun/ppermute | solution.py:448
  2070.4 12.6 select_add_fusion.c_ref
  2083.0 358.1 %branch_1_fun.1 = f32[2048,2048]{1,0:T(8,128)} custom-call(f32[2048,2048]{1,0:T(8,128)} %select_add_fusion.c_ref), custom_call_target="tpu_custom_call" | custom-call | tf_op jit(solution)/shard_map/cond/branch_1_fun/pallas_call | solution.py:451
  2441.0 13.9 fusion
  2454.9 0.5 collective-permute-start.7
  2455.4 43.3 %collective-permute-done.7 = f32[256,2048]{1,0:T(8,128)} collective-permute-done((f32[256,2048]{1,0:T(8,128)}, f32[256,2048]{1,0:T(8,128)}, u32[]{:S(2)}, u32[]{:S(2)}) %collective-permute-start.7) | collective-permute-done | bytes 2097184 | tf_op jit(solution)/shard_map/cond/branch_1_fun/ppermute | solution.py:439
  2498.7 17.1 fusion.6
  2515.8 1.1 constant_dynamic-slice_fusion
  2516.9 0.3 collective-permute-start.8
  2517.2 20.0 collective-permute-done.8
  2537.1 1.6 dynamic-slice_select_fusion
  2538.9 0.0 copy-start.1
  2538.9 2.4 copy.16
  2541.3 2.3 copy.17
  2543.6 0.0 copy-done.1
Async XLA Ops:
  0.6 1.6 copy-start
  0.6 8.0 copy-start.2
  0.7 8.0 copy-start.3
  160.5 13.5 collective-permute-start
  176.4 25.4 collective-permute-start.1
  213.9 364.1 %collective-permute-start.2 = (f32[2048,2048]{1,0:T(8,128)}, f32[2048,2048]{1,0:T(8,128)}, u32[]{:S(2)}, u32[]{:S(2)}) collective-permute-start(f32[2048,2048]{1,0:T(8,128)} %add.26), channel_id=1, source_target_pairs={{0,4},{2,6},{4,0},{6,2},{8,12},{10,14},{12,8},{14,10},{16,20},{18,... | collective-permute-start | bytes 50331656 | tf_op jit(solution)/shard_map/cond/branch_1_fun/ppermute | solution.py:448
  589.6 361.6 %collective-permute-start.3 = (f32[2048,2048]{1,0:T(8,128)S(1)}, f32[2048,2048]{1,0:T(8,128)}, u32[]{:S(2)}, u32[]{:S(2)}) collective-permute-start(f32[2048,2048]{1,0:T(8,128)S(1)} %add.27), channel_id=1, source_target_pairs={{0,8},{2,10},{4,12},{6,14},{8,0},{10,2},{12,4},{14,6},{16,24},{18,... | collective-permute-start | bytes 50331656 | tf_op jit(solution)/shard_map/cond/branch_1_fun/ppermute | solution.py:448
  963.4 362.3 %collective-permute-start.4 = (f32[2048,2048]{1,0:T(8,128)}, f32[2048,2048]{1,0:T(8,128)}, u32[]{:S(2)}, u32[]{:S(2)}) collective-permute-start(f32[2048,2048]{1,0:T(8,128)} %add.28), channel_id=1, source_target_pairs={{0,16},{2,18},{4,20},{6,22},{8,24},{10,26},{12,28},{14,30},{16,0},... | collective-permute-start | bytes 50331656 | tf_op jit(solution)/shard_map/cond/branch_1_fun/ppermute | solution.py:448
  1337.4 360.1 %collective-permute-start.5 = (f32[2048,2048]{1,0:T(8,128)S(1)}, f32[2048,2048]{1,0:T(8,128)}, u32[]{:S(2)}, u32[]{:S(2)}) collective-permute-start(f32[2048,2048]{1,0:T(8,128)S(1)} %add.29), channel_id=1, source_target_pairs={{0,32},{2,34},{4,36},{6,38},{8,40},{10,42},{12,44},{14,46},{16,48}... | collective-permute-start | bytes 50331656 | tf_op jit(solution)/shard_map/cond/branch_1_fun/ppermute | solution.py:448
  1709.6 360.8 %collective-permute-start.6 = (f32[2048,2048]{1,0:T(8,128)}, f32[2048,2048]{1,0:T(8,128)S(1)}, u32[]{:S(2)}, u32[]{:S(2)}) collective-permute-start(f32[2048,2048]{1,0:T(8,128)} %add.30), channel_id=1, source_target_pairs={{0,64},{2,66},{4,68},{6,70},{8,72},{10,74},{12,76},{14,78},{16,80}... | collective-permute-start | bytes 50331656 | tf_op jit(solution)/shard_map/cond/branch_1_fun/ppermute | solution.py:448
  2454.9 43.8 %collective-permute-start.7 = (f32[256,2048]{1,0:T(8,128)}, f32[256,2048]{1,0:T(8,128)}, u32[]{:S(2)}, u32[]{:S(2)}) collective-permute-start(f32[256,2048]{1,0:T(8,128)} %fusion), channel_id=1, source_target_pairs={{0,1},{1,0},{2,3},{3,2},{4,5},{5,4},{6,7},{7,6},{8,9},{9,8},{10,11... | collective-permute-start | bytes 6291464 | tf_op jit(solution)/shard_map/cond/branch_1_fun/ppermute | solution.py:439
  2516.9 20.3 collective-permute-start.8
  2538.9 4.8 copy-start.1

commit v3 on v2

--- a/solution.py
+++ b/solution.py
@@ -64,18 +64,17 @@
 
 
 def step_kernel(
-    total, ridge, h_ref, text_ref, quant_ref, flag_ref,
-    feat, part, arrived, mine, cov, lh, ll, g, a_scr, m_scr, wh, wl, w_send, w_recv, gh, gl, num, back, returned, bad, bad2,
-    e_send, e_recv, s_send, s_recv, x_send, x_recv, v_send, v_recv, u_send, u_recv, t_send, t_recv, w_s, w_r, b_s, b_r,
+    total, ridge, text_emb, quant_emb, text_head, quant_head, text_ref, quant_ref, flag_ref,
+    feat, away_feat, part, arrived, mine, cov, lh, ll, g, a_scr, m_scr, wh, wl, w_send, w_recv, gh, gl, num, back, returned, bad, bad2,
+    h_sem, e_send, e_recv, s_send, s_recv, x_send, x_recv, v_send, v_recv, u_send, u_recv, t_send, t_recv, w_s, w_r, b_s, b_r,
 ):
     at = lax.axis_index("rows")
     view = lax.axis_index("blk")
     core, xh, y, z = lax.rem(at, 2), lax.rem(at // 2, 2), lax.rem(at // 4, 4), at // 16
     twin = at + 1 - 2 * core
-    half_cols = h_ref.shape[2]
     peers = arrived.shape[0]
     nb = lh.shape[0] // B
-    per = half_cols // B
+    per = nb // 2
     starts = [sum(nb - c for c in range(k)) for k in range(nb)]
     order = [(i, j) for j in range(nb) for i in range(j, nb)]
     u, v = z + core * (y - z), y + core * (z - y)
@@ -89,30 +88,87 @@
 
     me = (u * 4 + v) * 2 + xh
 
+    depth = text_emb.shape[1] // 2
+    places = ((wh, wl, lh), (gh, gl, ll))
+
+    def for_view(which, text, quant):
+        @pl.when(view == 1 - which)
+        def _():
+            text()
+
+        @pl.when(view == which)
+        def _():
+            quant()
+
+    def emb_copy(src, which, half):
+        part_of = src.at[:, half * depth : (half + 1) * depth]
+        return pltpu.make_async_copy(part_of, places[which][half], h_sem.at[which, 2 * per + half])
+
+    def head_copy(src, which, half, c):
+        part_of = src.at[half * depth : (half + 1) * depth, c * B : (c + 1) * B]
+        at_cols = slice((half * per + c) * B, (half * per + c + 1) * B)
+        return pltpu.make_async_copy(part_of, places[which][2].at[:, at_cols], h_sem.at[which, 2 * c + half])
+
+    def fetch(which, emb, head):
+        for half in range(2):
+            emb_copy(emb, which, half).start()
+        for c in range(per):
+            for half in range(2):
+                head_copy(head, which, half, c).start()
+
+    for which in range(2):
+        for_view(which, lambda: fetch(which, text_emb, text_head), lambda: fetch(which, quant_emb, quant_head))
+
     barrier = pltpu.get_barrier_semaphore()
 
     def greet(d, _):
         pl.semaphore_signal(barrier, inc=1, device_id={"rows": device_of(lax.rem(me + d, peers))}, device_id_type=MESH)
         return 0
 
+    pl.semaphore_signal(barrier, inc=1, device_id={"blk": 1 - view}, device_id_type=MESH)
+    pl.semaphore_signal(barrier, inc=1, device_id={"rows": twin}, device_id_type=MESH)
     lax.fori_loop(1, peers, greet, 0)
-    pl.semaphore_signal(barrier, inc=1, device_id={"rows": twin}, device_id_type=MESH)
-    pl.semaphore_signal(barrier, inc=1, device_id={"blk": 1 - view}, device_id_type=MESH)
-    pl.semaphore_wait(barrier, peers + 1)
-
-    swap = push(h_ref.at[1 - view], feat.at[core, view], e_send.at[0], e_recv.at[0], blk=1 - view)
-    swap.start()
-    first = push(h_ref.at[view], feat.at[core, view], e_send.at[1], e_recv.at[1], rows=twin)
-    first.start()
-    feat[core, view] = h_ref[view]
-    swap.wait()
-    second = push(feat.at[core, 1 - view], feat.at[core, 1 - view], e_send.at[2], e_recv.at[2], rows=twin)
-    second.start()
-    first.wait()
-    second.wait()
-
-    def cols(b):
-        return lax.div(b, per), pl.ds(pl.multiple_of(lax.rem(b, per) * B, B), B)
+
+    def project(which, c):
+        emb0, emb1, head = places[which]
+        for half in range(2):
+            head_copy(text_head, which, half, c).wait()
+        lo, hi = slice(c * B, (c + 1) * B), slice((per + c) * B, (per + c + 1) * B)
+        return (mm(emb0[...], head[:, lo], NN) + mm(emb1[...], head[:, hi], NN)).astype(jnp.bfloat16)
+
+    sent = []
+
+    def go(copy):
+        copy.start()
+        sent.append(copy)
+
+    def swap(c, which_view):
+        return push(away_feat.at[c], feat.at[core, which_view * per + c], e_send.at[0, c], e_recv.at[0, c], blk=1 - view)
+
+    def share(turn, which_core, b):
+        c = lax.rem(b, per)
+        block = feat.at[which_core, b]
+        return push(block, block, e_send.at[turn, c], e_recv.at[turn, c], rows=twin)
+
+    for which in range(2):
+        for half in range(2):
+            emb_copy(text_emb, which, half).wait()
+        for c in range(per):
+            if which == 0:
+                away_feat[c] = project(which, c)
+                if c == 0:
+                    pl.semaphore_wait(barrier, peers + 1)
+                go(swap(c, view))
+            else:
+                feat[core, view * per + c] = project(which, c)
+                go(share(1, core, view * per + c))
+    for c in range(per):
+        swap(c, 1 - view).wait_recv()
+        go(share(2, core, (1 - view) * per + c))
+    for c in range(per):
+        share(1, 1 - core, view * per + c).wait_recv()
+    for c in range(per):
+        share(2, 1 - core, (1 - view) * per + c).wait_recv()
 
     offset = 0
     spans = []
@@ -121,8 +177,8 @@
         spans.append((begin, count, offset, rg))
         for t in range(count):
             (i0, j0), (i1, j1) = order[begin + t], order[begin + count + t]
-            (hi, ci), (hj, cj) = cols(i0 + core * (i1 - i0)), cols(j0 + core * (j1 - j0))
-            block = mm(feat[0, hi, :, ci], feat[0, hj, :, cj], TN) + mm(feat[1, hi, :, ci], feat[1, hj, :, cj], TN)
+            i, j = i0 + core * (i1 - i0), j0 + core * (j1 - j0)
+            block = mm(feat[0, i], feat[0, j], TN) + mm(feat[1, i], feat[1, j], TN)
             n = B // rg
             part[t * n : (t + 1) * n, offset : offset + rg] = block.astype(jnp.bfloat16).reshape(n, rg, B)
         offset += rg
@@ -160,12 +216,6 @@
 
     def same(rows, send, recv, dev):
         return push(cov.at[rows], cov.at[rows], send, recv, rows=dev)
-
-    sent = []
-
-    def go(copy):
-        copy.start()
-        sent.append(copy)
 
     def over_x(s, piece):
         return same(rows_at(s, core, piece, 1), x_send.at[s], x_recv.at[s], device(u, v, 1 - xh))
@@ -224,42 +274,61 @@
     relay(0)
     far(late)
     needs = {0: 0, 1: 1, 2: 2, 3: 3, 5: 4}
-    for k in range(nb):
-        if k in needs:
-            ready(needs[k])
+
+    def remainder(i, k):
+        first = (starts[k] - k + i) * B
+        value = cov[pl.ds(first if isinstance(i, int) else pl.multiple_of(first, B), B)]
+        if k:
+            ib = pl.ds(i * B if isinstance(i, int) else pl.multiple_of(i * B, B), B)
+            kb, done = slice(k * B, (k + 1) * B), slice(0, k * B)
+            value = value - dot3((lh[ib, done], ll[ib, done]), (lh[kb, done], ll[kb, done]), NT)
+        return value
+
+    def panel(i, k):
+        ib, kb = slice(i * B, (i + 1) * B), slice(k * B, (k + 1) * B)
+        lh[ib, kb], ll[ib, kb] = halves(dot3(halves(g[i]), (lh[kb, kb], ll[kb, kb]), NT))
+
+    def pivot(k):
+        kb = slice(k * B, (k + 1) * B)
+        inverse_factor(g.at[k], a_scr, m_scr, bad)
+        lh[kb, kb], ll[kb, kb] = halves(m_scr[...])
+
+    def whiten(k):
         kb, done = slice(k * B, (k + 1) * B), slice(0, k * B)
-
-        def left(i, _):
-            value = cov[pl.ds(pl.multiple_of((starts[k] - k + i) * B, B), B)]
-            if k:
-                ib = pl.ds(pl.multiple_of(i * B, B), B)
-                value = value - dot3((lh[ib, done], ll[ib, done]), (lh[kb, done], ll[kb, done]), NT)
-            g[i] = value
-            return 0
-
-        lax.fori_loop(k, nb, left, 0)
-        g[k] = g[k] + jnp.where(rows == lanes, ridge, 0.0)
-        inverse_factor(g.at[k], a_scr, m_scr, bad)
-        mk = halves(m_scr[...])
-        lh[kb, kb], ll[kb, kb] = mk
-        if k + 1 < len(spans):
-            relay(k + 1)
-
-        def panel(i, _):
-            ib = pl.ds(pl.multiple_of(i * B, B), B)
-            lh[ib, kb], ll[ib, kb] = halves(dot3(halves(g[i]), (lh[kb, kb], ll[kb, kb]), NT))
-            return 0
-
-        if k < nb - 1:
-            lax.fori_loop(k + 1, nb, panel, 0)
-        f = feat[core, k // per, :, (k % per) * B : (k % per + 1) * B].astype(jnp.float32)
+        f = feat[core, k].astype(jnp.float32)
         if k:
             f = f - dot3((wh[:, done], wl[:, done]), (lh[kb, done], ll[kb, done]), NT)
-        whi, wlo = halves(dot3(halves(f), mk, NT))
+        whi, wlo = halves(dot3(halves(f), (lh[kb, kb], ll[kb, kb]), NT))
         w_send[k] = whi
         if k < nb - 1:
             wh[:, kb], wl[:, kb] = whi, wlo
+
+    ready(0)
+    diagonal = jnp.where(rows == lanes, ridge, 0.0)
+    g[0] = remainder(0, 0) + diagonal
+    for i in range(1, nb):
+        g[i] = remainder(i, 0)
+    pivot(0)
+    for k in range(nb):
+        if k + 1 < len(spans):
+            relay(k + 1)
+        if k < nb - 1:
+            panel(k + 1, k)
+            if k + 1 in needs:
+                ready(needs[k + 1])
+            g[k + 1] = remainder(k + 1, k + 1) + diagonal
+            pivot(k + 1)
+            for i in range(k + 2, nb):
+                panel(i, k)
+        whiten(k)
         go(push(w_send.at[k], w_recv.at[k], w_s.at[k], w_r.at[k], blk=1 - view))
+
+        def left(i, _):
+            g[i] = remainder(i, k + 1)
+            return 0
+
+        if k < nb - 2:
+            lax.fori_loop(k + 2, nb, left, 0)
     flags = push(bad, bad2, w_s.at[nb], w_r.at[nb], blk=1 - view)
     flags.start()
 
@@ -301,9 +370,10 @@
         lax.fori_loop(1, peers, lambda d, _: (scatter(w, d).wait_send(), 0)[1], 0)
 
 
-def whole_step(h, peers, total):
-    _, rows, half = h.shape
-    n = 2 * half
+def whole_step(text_emb, quant_emb, text_head, quant_head, peers, total):
+    rows, emb = text_emb.shape
+    n = 2 * text_head.shape[1]
+    assert emb == 2 * n
     nb = n // B
     blocks = nb * (nb + 1) // 4
     chunk = blocks * B // peers
@@ -314,10 +384,11 @@
     return pl.pallas_call(
         functools.partial(step_kernel, total, ridge_weight),
         out_shape=[jax.ShapeDtypeStruct((rows // 2, n), f32)] * 2 + [jax.ShapeDtypeStruct((1,), f32)],
-        in_specs=[VMEM],
+        in_specs=[HBM] * 4,
         out_specs=[VMEM] * 2 + [pl.BlockSpec(memory_space=pltpu.SMEM)],
         scratch_shapes=[
-            pltpu.VMEM((2, 2, rows, half), bf),
+            pltpu.VMEM((2, nb, rows, B), bf),
+            pltpu.VMEM((nb // 2, rows, B), bf),
             pltpu.VMEM((peers, chunk, B), bf),
             pltpu.VMEM((peers, chunk, B), bf),
             pltpu.VMEM((chunk, B), f32),
@@ -338,8 +409,9 @@
             pltpu.VMEM((nb, rows // 2, B), bf),
             pltpu.VMEM((8, B), f32),
             pltpu.VMEM((8, B), f32),
-            dma((3,)),
-            dma((3,)),
+            dma((2, nb + 2)),
+            dma((3, nb // 2)),
+            dma((3, nb // 2)),
             dma((2, peers)),
             dma((2, peers)),
             dma((segs,)),
@@ -356,7 +428,7 @@
             dma((nb,)),
         ],
         compiler_params=pltpu.CompilerParams(collective_id=0, has_side_effects=True, vmem_limit_bytes=60 << 20),
-    )(h)
+    )(text_emb, quant_emb, text_head, quant_head)
 
 
 def direct_kernel(c_ref, m_ref, panel):
@@ -431,9 +503,15 @@
     lax.fori_loop(0, nb, step, 0)
 
 
-def direct_step(h, total):
+def direct_step(text_emb, quant_emb, text_head, quant_head, total):
     view = lax.axis_index("blk")
     ranks = lax.axis_size("rows")
+    h = jnp.stack(
+        [
+            jnp.dot(text_emb, text_head, preferred_element_type=jnp.float32).astype(jnp.bfloat16),
+            jnp.dot(quant_emb, quant_head, preferred_element_type=jnp.float32).astype(jnp.bfloat16),
+        ]
+    )
 
     def swapped(x):
         return lax.ppermute(x, "blk", [(0, 1), (1, 0)])
@@ -467,17 +545,11 @@
     return jnp.where(view == 0, own, other), jnp.where(view == 0, other, own)
 
 
-def shards(text_emb, quant_emb, text_head, quant_head):
+def shards(*arrays):
     peers = lax.axis_size("rows") // 2
-    total = text_emb.shape[0] * lax.axis_size("rows")
-    h = jnp.stack(
-        [
-            jnp.dot(text_emb, text_head, preferred_element_type=jnp.float32).astype(jnp.bfloat16),
-            jnp.dot(quant_emb, quant_head, preferred_element_type=jnp.float32).astype(jnp.bfloat16),
-        ]
-    )
-    text, quant, flag = whole_step(h, peers, total)
-    return lax.cond(flag[0] > 0, lambda: direct_step(h, total), lambda: (text, quant))
+    total = arrays[0].shape[0] * lax.axis_size("rows")
+    text, quant, flag = whole_step(*arrays, peers, total)
+    return lax.cond(flag[0] > 0, lambda: direct_step(*arrays, total), lambda: (text, quant))
 
 
 def solution(mesh):

time: 2550 us -> 2550 us (level)
  no operation moved by 1% of the time
where the time goes in v3:
time: 2550 us; the launch traced here: 2540 us
  waiting for transfers between devices  1910 us (75%)
  Pallas kernels  506 us (20%)
  other arithmetic  74.6 us (3%)
  matrix products  39.9 us (2%)
    ppermute x6, waiting for transfers between devices, direct_step(): cov = cov + lax.ppermute(cov, 'rows', [(r, r ^ hop) for r in range(ranks)])  1830 us
    pallas_call x1, Pallas kernels, direct_step(): pl.pallas_call(direct_kernel, out_shape=jax.ShapeDtypeStruct((n, n), jnp....  358 us
    pallas_call x1, Pallas kernels, whole_step(): pl.pallas_call(functools.partial(step_kernel, total, ridge_weight), out_s...  148 us
    ppermute x3, waiting for transfers between devices, swapped(): return lax.ppermute(x, 'blk', [(0, 1), (1, 0)])  75.2 us
    add x5, other arithmetic, direct_step(): cov = cov + lax.ppermute(cov, 'rows', [(r, r ^ hop) for r in range(ranks)])  60 us
  transfers between devices with their start and end apart: 9, of which 9 were waited for; matrix products, arithmetic and copies ran while one was open for 0% of the time, Pallas kernels for 0%

profile of v3, /device:TPU:0, one launch (start us, length us, event | category | flops | bytes accessed | tf_op | source)
XLA Modules:
  0.0 2539.3 jit_solution(13152993301712168581)
XLA Ops:
  0.6 0.0 copy-start.1
  0.6 148.0 %shard_map.63 = (f32[128,2048]{1,0:T(8,128)}, f32[128,2048]{1,0:T(8,128)}, f32[1]{0:T(128)}) custom-call(bf16[256,4096]{1,0:T(8,128)(2,1)} %text_emb.1, bf16[256,4096]{1,0:T(8,128)(2,1)} %quant_emb.1, bf16[4096,1024]{1,0:T(8,128)(2,1)} %text_head.1, bf16[4096,1024]{1,0:T(8,128)(2,1)} %quant_head.1), custom_call_target="tpu_custom_call" | custom-call | tf_op jit(solution)/shard_map/pallas_call | solution.py:384
  149.2 0.0 copy-done.1
  149.2 2385.2 %conditional.1 = ((f32[128,2048]{1,0:T(8,128)}, f32[128,2048]{1,0:T(8,128)})) conditional(s32[]{:T(128)} %bitcast.4, (f32[128,2048]{1,0:T(8,128)}, f32[128,2048]{1,0:T(8,128)}) %tuple.14, (bf16[256,4096]{1,0:T(8,128)(2,1)S(1)}, bf16[4096,1024]{1,0:T(8,128)(2,1)}, bf16[256,4096]{1,0:T(8,128)(2,1)}, bf16[4096,1024]{1,0:T(8,128)(2,1)}) %tuple.28), branch_computations={%region_0.0_spmd, %region_1.2_spmd} | conditional | flops 32265207808 | bytes 850395520 | solution.py:552
  149.2 0.0 copy-start
  149.3 0.0 copy-start.2
  149.3 5.9 fusion
  155.1 0.0 copy-done
  155.1 0.5 copy-done.2
  155.6 2.4 fusion.1
  158.0 0.4 fusion.5
  158.4 0.7 collective-permute-start
  159.1 13.3 collective-permute-done
  172.4 2.4 fusion.7
  174.9 0.1 collective-permute-start.1
  174.9 25.3 collective-permute-done.1
  200.2 12.1 add.26
  212.4 0.7 collective-permute-start.2
  213.1 363.4 %collective-permute-done.2 = f32[2048,2048]{1,0:T(8,128)} collective-permute-done((f32[2048,2048]{1,0:T(8,128)}, f32[2048,2048]{1,0:T(8,128)}, u32[]{:S(2)}, u32[]{:S(2)}) %collective-permute-start.2) | collective-permute-done | bytes 16777248 | tf_op jit(solution)/shard_map/cond/branch_1_fun/ppermute | solution.py:526
  576.4 11.6 add.27
  588.1 0.1 collective-permute-start.3
  588.2 361.5 %collective-permute-done.3 = f32[2048,2048]{1,0:T(8,128)} collective-permute-done((f32[2048,2048]{1,0:T(8,128)S(1)}, f32[2048,2048]{1,0:T(8,128)}, u32[]{:S(2)}, u32[]{:S(2)}) %collective-permute-start.3) | collective-permute-done | bytes 16777248 | tf_op jit(solution)/shard_map/cond/branch_1_fun/ppermute | solution.py:526
  949.7 12.5 add.28
  962.2 0.9 collective-permute-start.4
  963.1 361.5 %collective-permute-done.4 = f32[2048,2048]{1,0:T(8,128)} collective-permute-done((f32[2048,2048]{1,0:T(8,128)}, f32[2048,2048]{1,0:T(8,128)}, u32[]{:S(2)}, u32[]{:S(2)}) %collective-permute-start.4) | collective-permute-done | bytes 16777248 | tf_op jit(solution)/shard_map/cond/branch_1_fun/ppermute | solution.py:526
  1324.6 11.6 add.29
  1336.2 0.8 collective-permute-start.5
  1337.0 359.0 %collective-permute-done.5 = f32[2048,2048]{1,0:T(8,128)} collective-permute-done((f32[2048,2048]{1,0:T(8,128)S(1)}, f32[2048,2048]{1,0:T(8,128)}, u32[]{:S(2)}, u32[]{:S(2)}) %collective-permute-start.5) | collective-permute-done | bytes 16777248 | tf_op jit(solution)/shard_map/cond/branch_1_fun/ppermute | solution.py:526
  1696.0 12.1 add.30
  1708.1 0.8 collective-permute-start.6
  1708.9 359.6 %collective-permute-done.6 = f32[2048,2048]{1,0:T(8,128)S(1)} collective-permute-done((f32[2048,2048]{1,0:T(8,128)}, f32[2048,2048]{1,0:T(8,128)S(1)}, u32[]{:S(2)}, u32[]{:S(2)}) %collective-permute-start.6) | collective-permute-done | bytes 16777248 | tf_op jit(solution)/shard_map/cond/branch_1_fun/ppermute | solution.py:526
  2068.5 12.6 select_add_fusion.c_ref
  2081.1 358.1 %branch_1_fun.1 = f32[2048,2048]{1,0:T(8,128)} custom-call(f32[2048,2048]{1,0:T(8,128)} %select_add_fusion.c_ref), custom_call_target="tpu_custom_call" | custom-call | tf_op jit(solution)/shard_map/cond/branch_1_fun/pallas_call | solution.py:529
  2439.1 12.0 fusion.6
  2451.1 0.7 collective-permute-start.7
  2451.9 42.6 %collective-permute-done.7 = f32[256,2048]{1,0:T(8,128)} collective-permute-done((f32[256,2048]{1,0:T(8,128)S(1)}, f32[256,2048]{1,0:T(8,128)}, u32[]{:S(2)}, u32[]{:S(2)}) %collective-permute-start.7) | collective-permute-done | bytes 2097184 | tf_op jit(solution)/shard_map/cond/branch_1_fun/ppermute | solution.py:517
  2494.5 17.2 fusion.10
  2511.7 1.1 constant_dynamic-slice_fusion
  2512.8 0.7 collective-permute-start.8
  2513.4 19.3 collective-permute-done.8
  2532.8 1.5 dynamic-slice_select_fusion
  2534.5 2.3 copy.16
  2536.8 2.3 copy.17
Async XLA Ops:
  0.6 148.6 %copy-start.1 = (bf16[256,4096]{1,0:T(8,128)(2,1)S(1)}, bf16[256,4096]{1,0:T(8,128)(2,1)}, u32[]{:S(2)}) copy-start(bf16[256,4096]{1,0:T(8,128)(2,1)} %text_emb.1) | copy-start | bytes 6291460
  149.2 5.9 copy-start
  149.3 6.4 copy-start.2
  158.4 14.0 collective-permute-start
  174.9 25.4 collective-permute-start.1
  212.4 364.1 %collective-permute-start.2 = (f32[2048,2048]{1,0:T(8,128)}, f32[2048,2048]{1,0:T(8,128)}, u32[]{:S(2)}, u32[]{:S(2)}) collective-permute-start(f32[2048,2048]{1,0:T(8,128)} %add.26), channel_id=1, source_target_pairs={{0,4},{2,6},{4,0},{6,2},{8,12},{10,14},{12,8},{14,10},{16,20},{18,... | collective-permute-start | bytes 50331656 | tf_op jit(solution)/shard_map/cond/branch_1_fun/ppermute | solution.py:526
  588.1 361.6 %collective-permute-start.3 = (f32[2048,2048]{1,0:T(8,128)S(1)}, f32[2048,2048]{1,0:T(8,128)}, u32[]{:S(2)}, u32[]{:S(2)}) collective-permute-start(f32[2048,2048]{1,0:T(8,128)S(1)} %add.27), channel_id=1, source_target_pairs={{0,8},{2,10},{4,12},{6,14},{8,0},{10,2},{12,4},{14,6},{16,24},{18,... | collective-permute-start | bytes 50331656 | tf_op jit(solution)/shard_map/cond/branch_1_fun/ppermute | solution.py:526
  962.2 362.3 %collective-permute-start.4 = (f32[2048,2048]{1,0:T(8,128)}, f32[2048,2048]{1,0:T(8,128)}, u32[]{:S(2)}, u32[]{:S(2)}) collective-permute-start(f32[2048,2048]{1,0:T(8,128)} %add.28), channel_id=1, source_target_pairs={{0,16},{2,18},{4,20},{6,22},{8,24},{10,26},{12,28},{14,30},{16,0},... | collective-permute-start | bytes 50331656 | tf_op jit(solution)/shard_map/cond/branch_1_fun/ppermute | solution.py:526
  1336.2 359.8 %collective-permute-start.5 = (f32[2048,2048]{1,0:T(8,128)S(1)}, f32[2048,2048]{1,0:T(8,128)}, u32[]{:S(2)}, u32[]{:S(2)}) collective-permute-start(f32[2048,2048]{1,0:T(8,128)S(1)} %add.29), channel_id=1, source_target_pairs={{0,32},{2,34},{4,36},{6,38},{8,40},{10,42},{12,44},{14,46},{16,48}... | collective-permute-start | bytes 50331656 | tf_op jit(solution)/shard_map/cond/branch_1_fun/ppermute | solution.py:526
  1708.1 360.4 %collective-permute-start.6 = (f32[2048,2048]{1,0:T(8,128)}, f32[2048,2048]{1,0:T(8,128)S(1)}, u32[]{:S(2)}, u32[]{:S(2)}) collective-permute-start(f32[2048,2048]{1,0:T(8,128)} %add.30), channel_id=1, source_target_pairs={{0,64},{2,66},{4,68},{6,70},{8,72},{10,74},{12,76},{14,78},{16,80}... | collective-permute-start | bytes 50331656 | tf_op jit(solution)/shard_map/cond/branch_1_fun/ppermute | solution.py:526
  2451.1 43.3 %collective-permute-start.7 = (f32[256,2048]{1,0:T(8,128)S(1)}, f32[256,2048]{1,0:T(8,128)}, u32[]{:S(2)}, u32[]{:S(2)}) collective-permute-start(f32[256,2048]{1,0:T(8,128)S(1)} %fusion.6), channel_id=1, source_target_pairs={{0,1},{1,0},{2,3},{3,2},{4,5},{5,4},{6,7},{7,6},{8,9},{9,8},{10,11... | collective-permute-start | bytes 6291464 | tf_op jit(solution)/shard_map/cond/branch_1_fun/ppermute | solution.py:517
  2512.8 20.0 collective-permute-start.8

commit v4 on v3

--- a/solution.py
+++ b/solution.py
@@ -40,7 +40,7 @@
 EARLY = 2
 
 
-def inverse_factor(s_ref, a_ref, m_ref, bad_ref):
+def inverse_factor(s_ref, m_ref, bad_ref):
     rows = lax.broadcasted_iota(jnp.int32, (B, B), 0)
     cols = lax.broadcasted_iota(jnp.int32, (B, B), 1)
     eye = jnp.where(rows == cols, 1.0, 0.0)
@@ -52,20 +52,24 @@
     a = jnp.where(rows == cols, 1.0, s * sc * sr)
     step = eye - weight * (a - eye)
     m_ref[...] = step * sr
-    a_ref[...] = a
-    for turn in range(3):
-        t = halves(eye - weight * (a_ref[...] - eye))
-        if turn:
-            m_ref[...] = dot3(t, halves(m_ref[...]), NN)
-        a_ref[...] = dot3(halves(dot3(t, halves(a_ref[...]), NN)), t, NT)
-    gap = a_ref[...] - eye
-    bad_ref[...] += jnp.where(jnp.sum(gap * gap, axis=0, keepdims=True) <= 2.5e-5, 0.0, 1.0)
+    bf = jnp.bfloat16
+    t = (eye - weight * (a - eye)).astype(bf)
+    a = mm(mm(t, a.astype(bf), NN).astype(bf), t, NT)
+    t = (eye - weight * (a - eye)).astype(bf)
+    m_ref[...] = mm(t, m_ref[...].astype(bf), NN)
+    a = mm(mm(t, a.astype(bf), NN).astype(bf), t, NT)
+    t = (eye - weight * (a - eye)).astype(bf)
+    m_ref[...] = mm(t, m_ref[...].astype(bf), NN)
+    t = halves(m_ref[...])
+    gap = dot3(halves(dot3(t, halves(s_ref[...]), NN)), t, NT) - eye
+    far_off = jnp.sum(jnp.sum(gap * gap, axis=0, keepdims=True), axis=1, keepdims=True)
+    bad_ref[...] += jnp.where(far_off <= 0.06, 0.0, 1.0)
     m_ref[...] = dot3(halves(eye - weight * gap), halves(m_ref[...]), NN)
 
 
 def step_kernel(
     total, ridge, text_emb, quant_emb, text_head, quant_head, text_ref, quant_ref, flag_ref,
-    feat, away_feat, part, arrived, mine, cov, lh, ll, g, a_scr, m_scr, wh, wl, w_send, w_recv, gh, gl, num, back, returned, bad, bad2,
+    feat, away_feat, part, arrived, mine, cov, lh, ll, g, m_scr, wh, wl, w_send, w_recv, gh, gl, num, back, returned, bad, bad2,
     h_sem, e_send, e_recv, s_send, s_recv, x_send, x_recv, v_send, v_recv, u_send, u_recv, t_send, t_recv, w_s, w_r, b_s, b_r,
 ):
     at = lax.axis_index("rows")
@@ -290,7 +294,7 @@
 
     def pivot(k):
         kb = slice(k * B, (k + 1) * B)
-        inverse_factor(g.at[k], a_scr, m_scr, bad)
+        inverse_factor(g.at[k], m_scr, bad)
         lh[kb, kb], ll[kb, kb] = halves(m_scr[...])
 
     def whiten(k):
@@ -320,15 +324,10 @@
             pivot(k + 1)
             for i in range(k + 2, nb):
                 panel(i, k)
+        for i in range(k + 2, nb):
+            g[i] = remainder(i, k + 1)
         whiten(k)
         go(push(w_send.at[k], w_recv.at[k], w_s.at[k], w_r.at[k], blk=1 - view))
-
-        def left(i, _):
-            g[i] = remainder(i, k + 1)
-            return 0
-
-        if k < nb - 2:
-            lax.fori_loop(k + 2, nb, left, 0)
     flags = push(bad, bad2, w_s.at[nb], w_r.at[nb], blk=1 - view)
     flags.start()
 
@@ -396,7 +395,6 @@
             pltpu.VMEM((n, n), bf),
             pltpu.VMEM((n, n), bf),
             pltpu.VMEM((nb, B, B), f32),
-            pltpu.VMEM((B, B), f32),
             pltpu.VMEM((B, B), f32),
             pltpu.VMEM((rows, n), bf),
             pltpu.VMEM((rows, n), bf),
@@ -549,7 +547,7 @@
     peers = lax.axis_size("rows") // 2
     total = arrays[0].shape[0] * lax.axis_size("rows")
     text, quant, flag = whole_step(*arrays, peers, total)
-    return lax.cond(flag[0] > 0, lambda: direct_step(*arrays, total), lambda: (text, quant))
+    return lax.cond(flag[0] > 0, lambda: direct_step(*arrays, total), lambda: (text + flag[0], quant + flag[0]))
 
 
 def solution(mesh):

time: 2550 us -> 2530 us (level)
  no operation moved by 1% of the time
where the time goes in v4:
time: 2530 us
  waiting for transfers between devices  1910 us (75%)
  Pallas kernels  495 us (20%)
  other arithmetic  74.2 us (3%)
  matrix products  39.7 us (2%)
    ppermute x6, waiting for transfers between devices, direct_step(): cov = cov + lax.ppermute(cov, 'rows', [(r, r ^ hop) for r in range(ranks)])  1830 us
    pallas_call x1, Pallas kernels, direct_step(): pl.pallas_call(direct_kernel, out_shape=jax.ShapeDtypeStruct((n, n), jnp....  358 us
    pallas_call x1, Pallas kernels, whole_step(): pl.pallas_call(functools.partial(step_kernel, total, ridge_weight), out_s...  137 us
    ppermute x3, waiting for transfers between devices, swapped(): return lax.ppermute(x, 'blk', [(0, 1), (1, 0)])  76.3 us
    add x5, other arithmetic, direct_step(): cov = cov + lax.ppermute(cov, 'rows', [(r, r ^ hop) for r in range(ranks)])  59.7 us
  transfers between devices with their start and end apart: 9, of which 9 were waited for; matrix products, arithmetic and copies ran while one was open for 0% of the time, Pallas kernels for 0%

profile of v4, /device:TPU:0, one launch (start us, length us, event | category | flops | bytes accessed | tf_op | source)
XLA Modules:
  0.0 2525.1 jit_solution(7032971874053263854)
XLA Ops:
  0.6 0.0 copy-start.1
  0.6 137.4 %shard_map.63 = (f32[128,2048]{1,0:T(8,128)S(1)}, f32[128,2048]{1,0:T(8,128)}, f32[1]{0:T(128)}) custom-call(bf16[256,4096]{1,0:T(8,128)(2,1)} %text_emb.1, bf16[256,4096]{1,0:T(8,128)(2,1)} %quant_emb.1, bf16[4096,1024]{1,0:T(8,128)(2,1)} %text_head.1, bf16[4096,1024]{1,0:T(8,128)(2,1)} %quant_head.1), custom_call_target="tpu_custom_call" | custom-call | tf_op jit(solution)/shard_map/pallas_call | solution.py:383
  138.7 0.0 copy-done.1
  138.7 2385.0 %conditional.1 = (f32[128,2048]{1,0:T(8,128)}, f32[128,2048]{1,0:T(8,128)}) conditional(s32[]{:T(128)} %bitcast.5, (f32[1]{0:T(128)}, f32[128,2048]{1,0:T(8,128)S(1)}, f32[128,2048]{1,0:T(8,128)}) %tuple.15, (bf16[256,4096]{1,0:T(8,128)(2,1)S(1)}, bf16[4096,1024]{1,0:T(8,128)(2,1)}, bf16[256,4096]{1,0:T(8,128)(2,1)}, ...), branch_computations={%region_0.0_spmd, %region_1.2_spmd} | conditional | flops 32265207808 | bytes 850395520 | solution.py:550
  138.8 0.0 copy-start
  138.8 0.0 copy-start.2
  138.8 5.9 fusion
  144.7 0.0 copy-done
  144.7 0.5 copy-done.2
  145.1 2.4 fusion.1
  147.5 0.4 fusion.5
  147.9 0.3 collective-permute-start
  148.2 13.7 collective-permute-done
  161.9 2.4 fusion.7
  164.3 0.1 collective-permute-start.1
  164.4 25.3 %collective-permute-done.1 = f32[2048,2048]{1,0:T(8,128)} collective-permute-done((f32[2048,2048]{1,0:T(8,128)S(1)}, f32[2048,2048]{1,0:T(8,128)}, u32[]{:S(2)}, u32[]{:S(2)}) %collective-permute-start.1) | collective-permute-done | bytes 16777248 | tf_op jit(solution)/shard_map/cond/branch_1_fun/ppermute | solution.py:524
  189.7 12.1 add.36
  201.8 1.2 collective-permute-start.2
  203.0 362.9 %collective-permute-done.2 = f32[2048,2048]{1,0:T(8,128)} collective-permute-done((f32[2048,2048]{1,0:T(8,128)}, f32[2048,2048]{1,0:T(8,128)}, u32[]{:S(2)}, u32[]{:S(2)}) %collective-permute-start.2) | collective-permute-done | bytes 16777248 | tf_op jit(solution)/shard_map/cond/branch_1_fun/ppermute | solution.py:524
  565.9 11.6 add.37
  577.6 0.1 collective-permute-start.3
  577.7 361.5 %collective-permute-done.3 = f32[2048,2048]{1,0:T(8,128)} collective-permute-done((f32[2048,2048]{1,0:T(8,128)S(1)}, f32[2048,2048]{1,0:T(8,128)}, u32[]{:S(2)}, u32[]{:S(2)}) %collective-permute-start.3) | collective-permute-done | bytes 16777248 | tf_op jit(solution)/shard_map/cond/branch_1_fun/ppermute | solution.py:524
  939.2 12.1 add.38
  951.3 1.1 collective-permute-start.4
  952.4 361.3 %collective-permute-done.4 = f32[2048,2048]{1,0:T(8,128)} collective-permute-done((f32[2048,2048]{1,0:T(8,128)}, f32[2048,2048]{1,0:T(8,128)}, u32[]{:S(2)}, u32[]{:S(2)}) %collective-permute-start.4) | collective-permute-done | bytes 16777248 | tf_op jit(solution)/shard_map/cond/branch_1_fun/ppermute | solution.py:524
  1313.7 11.6 add.39
  1325.3 0.7 collective-permute-start.5
  1326.0 359.1 %collective-permute-done.5 = f32[2048,2048]{1,0:T(8,128)} collective-permute-done((f32[2048,2048]{1,0:T(8,128)S(1)}, f32[2048,2048]{1,0:T(8,128)}, u32[]{:S(2)}, u32[]{:S(2)}) %collective-permute-start.5) | collective-permute-done | bytes 16777248 | tf_op jit(solution)/shard_map/cond/branch_1_fun/ppermute | solution.py:524
  1685.1 12.1 add.40
  1697.2 1.4 collective-permute-start.6
  1698.6 359.2 %collective-permute-done.6 = f32[2048,2048]{1,0:T(8,128)S(1)} collective-permute-done((f32[2048,2048]{1,0:T(8,128)}, f32[2048,2048]{1,0:T(8,128)S(1)}, u32[]{:S(2)}, u32[]{:S(2)}) %collective-permute-start.6) | collective-permute-done | bytes 16777248 | tf_op jit(solution)/shard_map/cond/branch_1_fun/ppermute | solution.py:524
  2057.8 12.6 select_add_fusion.c_ref
  2070.4 358.1 %branch_1_fun.1 = f32[2048,2048]{1,0:T(8,128)} custom-call(f32[2048,2048]{1,0:T(8,128)} %select_add_fusion.c_ref), custom_call_target="tpu_custom_call" | custom-call | tf_op jit(solution)/shard_map/cond/branch_1_fun/pallas_call | solution.py:527
  2428.5 12.0 fusion.6
  2440.5 0.4 collective-permute-start.7
  2440.8 43.0 %collective-permute-done.7 = f32[256,2048]{1,0:T(8,128)} collective-permute-done((f32[256,2048]{1,0:T(8,128)S(1)}, f32[256,2048]{1,0:T(8,128)}, u32[]{:S(2)}, u32[]{:S(2)}) %collective-permute-start.7) | collective-permute-done | bytes 2097184 | tf_op jit(solution)/shard_map/cond/branch_1_fun/ppermute | solution.py:515
  2483.8 17.1 fusion.10
  2500.9 1.1 constant_dynamic-slice_fusion
  2501.9 0.3 collective-permute-start.8
  2502.2 19.7 collective-permute-done.8
  2521.9 1.5 dynamic-slice_select_fusion
Async XLA Ops:
  0.6 138.1 %copy-start.1 = (bf16[256,4096]{1,0:T(8,128)(2,1)S(1)}, bf16[256,4096]{1,0:T(8,128)(2,1)}, u32[]{:S(2)}) copy-start(bf16[256,4096]{1,0:T(8,128)(2,1)} %text_emb.1) | copy-start | bytes 6291460
  138.8 5.9 copy-start
  138.8 6.4 copy-start.2
  147.9 14.0 collective-permute-start
  164.3 25.4 %collective-permute-start.1 = (f32[2048,2048]{1,0:T(8,128)S(1)}, f32[2048,2048]{1,0:T(8,128)}, u32[]{:S(2)}, u32[]{:S(2)}) collective-permute-start(f32[2048,2048]{1,0:T(8,128)S(1)} %fusion.7), channel_id=1, source_target_pairs={{0,2},{2,0},{4,6},{6,4},{8,10},{10,8},{12,14},{14,12},{16,18},{18,... | collective-permute-start | bytes 50331656 | tf_op jit(solution)/shard_map/cond/branch_1_fun/ppermute | solution.py:524
  201.8 364.1 %collective-permute-start.2 = (f32[2048,2048]{1,0:T(8,128)}, f32[2048,2048]{1,0:T(8,128)}, u32[]{:S(2)}, u32[]{:S(2)}) collective-permute-start(f32[2048,2048]{1,0:T(8,128)} %add.36), channel_id=1, source_target_pairs={{0,4},{2,6},{4,0},{6,2},{8,12},{10,14},{12,8},{14,10},{16,20},{18,... | collective-permute-start | bytes 50331656 | tf_op jit(solution)/shard_map/cond/branch_1_fun/ppermute | solution.py:524
  577.6 361.6 %collective-permute-start.3 = (f32[2048,2048]{1,0:T(8,128)S(1)}, f32[2048,2048]{1,0:T(8,128)}, u32[]{:S(2)}, u32[]{:S(2)}) collective-permute-start(f32[2048,2048]{1,0:T(8,128)S(1)} %add.37), channel_id=1, source_target_pairs={{0,8},{2,10},{4,12},{6,14},{8,0},{10,2},{12,4},{14,6},{16,24},{18,... | collective-permute-start | bytes 50331656 | tf_op jit(solution)/shard_map/cond/branch_1_fun/ppermute | solution.py:524
  951.3 362.3 %collective-permute-start.4 = (f32[2048,2048]{1,0:T(8,128)}, f32[2048,2048]{1,0:T(8,128)}, u32[]{:S(2)}, u32[]{:S(2)}) collective-permute-start(f32[2048,2048]{1,0:T(8,128)} %add.38), channel_id=1, source_target_pairs={{0,16},{2,18},{4,20},{6,22},{8,24},{10,26},{12,28},{14,30},{16,0},... | collective-permute-start | bytes 50331656 | tf_op jit(solution)/shard_map/cond/branch_1_fun/ppermute | solution.py:524
  1325.3 359.8 %collective-permute-start.5 = (f32[2048,2048]{1,0:T(8,128)S(1)}, f32[2048,2048]{1,0:T(8,128)}, u32[]{:S(2)}, u32[]{:S(2)}) collective-permute-start(f32[2048,2048]{1,0:T(8,128)S(1)} %add.39), channel_id=1, source_target_pairs={{0,32},{2,34},{4,36},{6,38},{8,40},{10,42},{12,44},{14,46},{16,48}... | collective-permute-start | bytes 50331656 | tf_op jit(solution)/shard_map/cond/branch_1_fun/ppermute | solution.py:524
  1697.2 360.6 %collective-permute-start.6 = (f32[2048,2048]{1,0:T(8,128)}, f32[2048,2048]{1,0:T(8,128)S(1)}, u32[]{:S(2)}, u32[]{:S(2)}) collective-permute-start(f32[2048,2048]{1,0:T(8,128)} %add.40), channel_id=1, source_target_pairs={{0,64},{2,66},{4,68},{6,70},{8,72},{10,74},{12,76},{14,78},{16,80}... | collective-permute-start | bytes 50331656 | tf_op jit(solution)/shard_map/cond/branch_1_fun/ppermute | solution.py:524
  2440.5 43.3 %collective-permute-start.7 = (f32[256,2048]{1,0:T(8,128)S(1)}, f32[256,2048]{1,0:T(8,128)}, u32[]{:S(2)}, u32[]{:S(2)}) collective-permute-start(f32[256,2048]{1,0:T(8,128)S(1)} %fusion.6), channel_id=1, source_target_pairs={{0,1},{1,0},{2,3},{3,2},{4,5},{5,4},{6,7},{7,6},{8,9},{9,8},{10,11... | collective-permute-start | bytes 6291464 | tf_op jit(solution)/shard_map/cond/branch_1_fun/ppermute | solution.py:515
  2501.9 20.0 collective-permute-start.8

commit v5 on v4

--- a/solution.py
+++ b/solution.py
@@ -70,7 +70,7 @@
 def step_kernel(
     total, ridge, text_emb, quant_emb, text_head, quant_head, text_ref, quant_ref, flag_ref,
     feat, away_feat, part, arrived, mine, cov, lh, ll, g, m_scr, wh, wl, w_send, w_recv, gh, gl, num, back, returned, bad, bad2,
-    h_sem, e_send, e_recv, s_send, s_recv, x_send, x_recv, v_send, v_recv, u_send, u_recv, t_send, t_recv, w_s, w_r, b_s, b_r,
+    h_sem, e_send, e_recv, s_send, s_recv, v_send, v_recv, u_send, u_recv, t_send, t_recv, w_s, w_r, b_s, b_r,
 ):
     at = lax.axis_index("rows")
     view = lax.axis_index("blk")
@@ -113,15 +113,19 @@
         at_cols = slice((half * per + c) * B, (half * per + c + 1) * B)
         return pltpu.make_async_copy(part_of, places[which][2].at[:, at_cols], h_sem.at[which, 2 * c + half])
 
-    def fetch(which, emb, head):
-        for half in range(2):
-            emb_copy(emb, which, half).start()
-        for c in range(per):
+    def fetch(turn):
+        which, c = turn // per, turn % per
+
+        def start(emb, head):
             for half in range(2):
+                if c == 0:
+                    emb_copy(emb, which, half).start()
                 head_copy(head, which, half, c).start()
 
-    for which in range(2):
-        for_view(which, lambda: fetch(which, text_emb, text_head), lambda: fetch(which, quant_emb, quant_head))
+        for_view(which, lambda: start(text_emb, text_head), lambda: start(quant_emb, quant_head))
+
+    for turn in range(2):
+        fetch(turn)
 
     barrier = pltpu.get_barrier_semaphore()
 
@@ -158,6 +162,8 @@
         for half in range(2):
             emb_copy(text_emb, which, half).wait()
         for c in range(per):
+            if which * per + c + 2 < 2 * per:
+                fetch(which * per + c + 2)
             if which == 0:
                 away_feat[c] = project(which, c)
                 if c == 0:
@@ -179,13 +185,16 @@
     for begin, count in SEGMENTS:
         rg = count * B // peers
         spans.append((begin, count, offset, rg))
-        for t in range(count):
-            (i0, j0), (i1, j1) = order[begin + t], order[begin + count + t]
-            i, j = i0 + core * (i1 - i0), j0 + core * (j1 - j0)
-            block = mm(feat[0, i], feat[0, j], TN) + mm(feat[1, i], feat[1, j], TN)
-            n = B // rg
-            part[t * n : (t + 1) * n, offset : offset + rg] = block.astype(jnp.bfloat16).reshape(n, rg, B)
         offset += rg
+
+    def products(segments):
+        for begin, count, off, rg in segments:
+            for t in range(count):
+                (i0, j0), (i1, j1) = order[begin + t], order[begin + count + t]
+                i, j = i0 + core * (i1 - i0), j0 + core * (j1 - j0)
+                block = mm(feat[0, i], feat[0, j], TN) + mm(feat[1, i], feat[1, j], TN)
+                n = B // rg
+                part[t * n : (t + 1) * n, off : off + rg] = block.astype(jnp.bfloat16).reshape(n, rg, B)
 
     cut = spans[EARLY][2]
     waves = [(0, cut), (cut, mine.shape[0] - cut)]
@@ -200,7 +209,8 @@
         piece = pl.ds(*waves[w])
         return push(part.at[p, piece], arrived.at[p, piece], s_send.at[w, d], s_recv.at[w, d], rows=device_of(p))
 
-    for w in range(2):
+    for w, segments in enumerate((spans[:EARLY], spans[EARLY:])):
+        products(segments)
         lax.fori_loop(1, peers, lambda d, _: (scatter(w, d).start(), 0)[1], 0)
 
     def reduce(w):
@@ -221,11 +231,9 @@
     def same(rows, send, recv, dev):
         return push(cov.at[rows], cov.at[rows], send, recv, rows=dev)
 
-    def over_x(s, piece):
-        return same(rows_at(s, core, piece, 1), x_send.at[s], x_recv.at[s], device(u, v, 1 - xh))
-
-    def over_v(s, d, pv):
-        return same(rows_at(s, core, (u * 4 + pv) * 2, 2), v_send.at[s, d], v_recv.at[s, d], device(u, lax.rem(v + d, 4), xh))
+    def close_by(s, d, piece):
+        there = device(u, lax.rem(v + d // 2, 4), lax.rem(xh + d, 2))
+        return same(rows_at(s, core, piece, 1), v_send.at[s, d], v_recv.at[s, d], there)
 
     def over_u(s, d, pu):
         return same(rows_at(s, core, pu * 8, 8), u_send.at[s, d], u_recv.at[s, d], device(lax.rem(u + d, 4), v, xh))
@@ -237,18 +245,14 @@
         for s in segments:
             _, _, off, rg = spans[s]
             cov[rows_at(s, core, me, 1)] = mine[off : off + rg] * (1.0 / total)
-            go(over_x(s, me))
-
-    def middle(segments):
-        for s in segments:
-            over_x(s, me + 1 - 2 * xh).wait_recv()
-            for d in range(1, 4):
-                go(over_v(s, d, v))
+            for d in range(1, 8):
+                go(close_by(s, d, me))
 
     def far(segments):
         for s in segments:
-            for d in range(1, 4):
-                over_v(s, d, lax.rem(v + 4 - d, 4)).wait_recv()
+            for d in range(1, 8):
+                from_there = (u * 4 + lax.rem(v + 4 - d // 2, 4)) * 2 + lax.rem(xh + d, 2)
+                close_by(s, d, from_there).wait_recv()
             for d in range(1, 4):
                 go(over_u(s, d, u))
             go(to_twin(s, 0, core, u))
@@ -270,11 +274,9 @@
     early, late = range(EARLY), range(EARLY, len(spans))
     reduce(0)
     near(early)
-    middle(early)
     far(early)
     reduce(1)
     near(late)
-    middle(late)
     relay(0)
     far(late)
     needs = {0: 0, 1: 1, 2: 2, 3: 3, 5: 4}
@@ -314,10 +316,11 @@
         g[i] = remainder(i, 0)
     pivot(0)
     for k in range(nb):
+        if k < nb - 1:
+            panel(k + 1, k)
         if k + 1 < len(spans):
             relay(k + 1)
         if k < nb - 1:
-            panel(k + 1, k)
             if k + 1 in needs:
                 ready(needs[k + 1])
             g[k + 1] = remainder(k + 1, k + 1) + diagonal
@@ -335,19 +338,21 @@
     own = pl.ds(pl.multiple_of(view * half, half), half)
     away = pl.ds(pl.multiple_of((1 - view) * half, half), half)
     for k in reversed(range(nb)):
-        kb, rest = slice(k * B, (k + 1) * B), slice((k + 1) * B, nb * B)
         push(w_send.at[k], w_recv.at[k], w_s.at[k], w_r.at[k], blk=1 - view).wait_recv()
-        value = w_recv[k].astype(jnp.float32)
-        if k < nb - 1:
-            value = value - dot3((gh[:, rest], gl[:, rest]), (lh[rest, kb], ll[rest, kb]), NN)
-        value = dot3(halves(value), (lh[kb, kb], ll[kb, kb]), NN)
-        if k:
-            gh[:, kb], gl[:, kb] = halves(value)
+    for k in reversed(range(nb)):
+        kb = slice(k * B, (k + 1) * B)
+        rest = w_recv[k].astype(jnp.float32) if k == nb - 1 else g[k]
+        value = dot3(halves(rest), (lh[kb, kb], ll[kb, kb]), NN)
         num[...] = value
         back[k] = num[away].astype(jnp.bfloat16)
         go(push(back.at[k], returned.at[k], b_s.at[k], b_r.at[k], blk=1 - view))
         text_ref[:, kb] = num[own]
         quant_ref[:, kb] = num[own]
+        found = halves(value)
+        for j in reversed(range(k)):
+            jb = slice(j * B, (j + 1) * B)
+            rest = w_recv[j].astype(jnp.float32) if k == nb - 1 else g[j]
+            g[j] = rest - dot3(found, (lh[kb, jb], ll[kb, jb]), NN)
     for k in reversed(range(nb)):
         kb = slice(k * B, (k + 1) * B)
         push(back.at[k], returned.at[k], b_s.at[k], b_r.at[k], blk=1 - view).wait_recv()
@@ -412,10 +417,8 @@
             dma((3, nb // 2)),
             dma((2, peers)),
             dma((2, peers)),
-            dma((segs,)),
-            dma((segs,)),
-            dma((segs, 4)),
-            dma((segs, 4)),
+            dma((segs, 8)),
+            dma((segs, 8)),
             dma((segs, 4)),
             dma((segs, 4)),
             dma((segs, 4)),

time: 2530 us -> 2530 us (level)
  no operation moved by 1% of the time
where the time goes in v5:
time: 2530 us; the launch traced here: 2520 us
  waiting for transfers between devices  1900 us (75%)
  Pallas kernels  494 us (20%)
  other arithmetic  74.4 us (3%)
  matrix products  39.7 us (2%)
    ppermute x6, waiting for transfers between devices, direct_step(): cov = cov + lax.ppermute(cov, 'rows', [(r, r ^ hop) for r in range(ranks)])  1830 us
    pallas_call x1, Pallas kernels, direct_step(): pl.pallas_call(direct_kernel, out_shape=jax.ShapeDtypeStruct((n, n), jnp....  358 us
    pallas_call x1, Pallas kernels, whole_step(): pl.pallas_call(functools.partial(step_kernel, total, ridge_weight), out_s...  136 us
    ppermute x3, waiting for transfers between devices, swapped(): return lax.ppermute(x, 'blk', [(0, 1), (1, 0)])  76.1 us
    add x5, other arithmetic, direct_step(): cov = cov + lax.ppermute(cov, 'rows', [(r, r ^ hop) for r in range(ranks)])  59.9 us
  transfers between devices with their start and end apart: 9, of which 9 were waited for; matrix products, arithmetic and copies ran while one was open for 0% of the time, Pallas kernels for 0%

profile of v5, /device:TPU:0, one launch (start us, length us, event | category | flops | bytes accessed | tf_op | source)
XLA Modules:
  0.0 2523.1 jit_solution(5875452913324932932)
XLA Ops:
  0.6 0.0 copy-start.1
  0.6 136.0 %shard_map.63 = (f32[128,2048]{1,0:T(8,128)S(1)}, f32[128,2048]{1,0:T(8,128)}, f32[1]{0:T(128)}) custom-call(bf16[256,4096]{1,0:T(8,128)(2,1)} %text_emb.1, bf16[256,4096]{1,0:T(8,128)(2,1)} %quant_emb.1, bf16[4096,1024]{1,0:T(8,128)(2,1)} %text_head.1, bf16[4096,1024]{1,0:T(8,128)(2,1)} %quant_head.1), custom_call_target="tpu_custom_call" | custom-call | tf_op jit(solution)/shard_map/pallas_call | solution.py:388
  137.3 0.0 copy-done.1
  137.3 2384.5 %conditional.1 = (f32[128,2048]{1,0:T(8,128)}, f32[128,2048]{1,0:T(8,128)}) conditional(s32[]{:T(128)} %bitcast.5, (f32[1]{0:T(128)}, f32[128,2048]{1,0:T(8,128)S(1)}, f32[128,2048]{1,0:T(8,128)}) %tuple.15, (bf16[256,4096]{1,0:T(8,128)(2,1)S(1)}, bf16[4096,1024]{1,0:T(8,128)(2,1)}, bf16[256,4096]{1,0:T(8,128)(2,1)}, ...), branch_computations={%region_0.0_spmd, %region_1.2_spmd} | conditional | flops 32265207808 | bytes 850395520 | solution.py:553
  137.4 0.0 copy-start
  137.4 0.0 copy-start.2
  137.4 5.9 fusion
  143.3 0.0 copy-done
  143.3 0.5 copy-done.2
  143.7 2.4 fusion.1
  146.1 0.4 fusion.5
  146.5 0.1 collective-permute-start
  146.6 13.5 collective-permute-done
  160.1 2.4 fusion.7
  162.5 0.1 collective-permute-start.1
  162.6 25.3 %collective-permute-done.1 = f32[2048,2048]{1,0:T(8,128)} collective-permute-done((f32[2048,2048]{1,0:T(8,128)S(1)}, f32[2048,2048]{1,0:T(8,128)}, u32[]{:S(2)}, u32[]{:S(2)}) %collective-permute-start.1) | collective-permute-done | bytes 16777248 | tf_op jit(solution)/shard_map/cond/branch_1_fun/ppermute | solution.py:527
  187.9 12.3 add.36
  200.2 1.2 collective-permute-start.2
  201.4 362.9 %collective-permute-done.2 = f32[2048,2048]{1,0:T(8,128)} collective-permute-done((f32[2048,2048]{1,0:T(8,128)}, f32[2048,2048]{1,0:T(8,128)}, u32[]{:S(2)}, u32[]{:S(2)}) %collective-permute-start.2) | collective-permute-done | bytes 16777248 | tf_op jit(solution)/shard_map/cond/branch_1_fun/ppermute | solution.py:527
  564.3 11.6 add.37
  576.0 0.8 collective-permute-start.3
  576.7 360.8 %collective-permute-done.3 = f32[2048,2048]{1,0:T(8,128)} collective-permute-done((f32[2048,2048]{1,0:T(8,128)S(1)}, f32[2048,2048]{1,0:T(8,128)}, u32[]{:S(2)}, u32[]{:S(2)}) %collective-permute-start.3) | collective-permute-done | bytes 16777248 | tf_op jit(solution)/shard_map/cond/branch_1_fun/ppermute | solution.py:527
  937.6 12.1 add.38
  949.7 1.6 collective-permute-start.4
  951.3 360.7 %collective-permute-done.4 = f32[2048,2048]{1,0:T(8,128)} collective-permute-done((f32[2048,2048]{1,0:T(8,128)}, f32[2048,2048]{1,0:T(8,128)}, u32[]{:S(2)}, u32[]{:S(2)}) %collective-permute-start.4) | collective-permute-done | bytes 16777248 | tf_op jit(solution)/shard_map/cond/branch_1_fun/ppermute | solution.py:527
  1312.0 11.6 add.39
  1323.7 0.1 collective-permute-start.5
  1323.8 359.7 %collective-permute-done.5 = f32[2048,2048]{1,0:T(8,128)} collective-permute-done((f32[2048,2048]{1,0:T(8,128)S(1)}, f32[2048,2048]{1,0:T(8,128)}, u32[]{:S(2)}, u32[]{:S(2)}) %collective-permute-start.5) | collective-permute-done | bytes 16777248 | tf_op jit(solution)/shard_map/cond/branch_1_fun/ppermute | solution.py:527
  1683.5 12.1 add.40
  1695.6 1.4 collective-permute-start.6
  1697.0 358.9 %collective-permute-done.6 = f32[2048,2048]{1,0:T(8,128)S(1)} collective-permute-done((f32[2048,2048]{1,0:T(8,128)}, f32[2048,2048]{1,0:T(8,128)S(1)}, u32[]{:S(2)}, u32[]{:S(2)}) %collective-permute-start.6) | collective-permute-done | bytes 16777248 | tf_op jit(solution)/shard_map/cond/branch_1_fun/ppermute | solution.py:527
  2056.0 12.6 select_add_fusion.c_ref
  2068.6 358.1 %branch_1_fun.1 = f32[2048,2048]{1,0:T(8,128)} custom-call(f32[2048,2048]{1,0:T(8,128)} %select_add_fusion.c_ref), custom_call_target="tpu_custom_call" | custom-call | tf_op jit(solution)/shard_map/cond/branch_1_fun/pallas_call | solution.py:530
  2426.6 12.0 fusion.6
  2438.6 0.4 collective-permute-start.7
  2439.0 43.0 %collective-permute-done.7 = f32[256,2048]{1,0:T(8,128)} collective-permute-done((f32[256,2048]{1,0:T(8,128)S(1)}, f32[256,2048]{1,0:T(8,128)}, u32[]{:S(2)}, u32[]{:S(2)}) %collective-permute-start.7) | collective-permute-done | bytes 2097184 | tf_op jit(solution)/shard_map/cond/branch_1_fun/ppermute | solution.py:518
  2482.0 17.1 fusion.10
  2499.1 1.1 constant_dynamic-slice_fusion
  2500.1 0.3 collective-permute-start.8
  2500.4 19.7 collective-permute-done.8
  2520.1 1.5 dynamic-slice_select_fusion
Async XLA Ops:
  0.6 136.7 %copy-start.1 = (bf16[256,4096]{1,0:T(8,128)(2,1)S(1)}, bf16[256,4096]{1,0:T(8,128)(2,1)}, u32[]{:S(2)}) copy-start(bf16[256,4096]{1,0:T(8,128)(2,1)} %text_emb.1) | copy-start | bytes 6291460
  137.4 5.9 copy-start
  137.4 6.4 copy-start.2
  146.5 13.6 collective-permute-start
  162.5 25.4 %collective-permute-start.1 = (f32[2048,2048]{1,0:T(8,128)S(1)}, f32[2048,2048]{1,0:T(8,128)}, u32[]{:S(2)}, u32[]{:S(2)}) collective-permute-start(f32[2048,2048]{1,0:T(8,128)S(1)} %fusion.7), channel_id=1, source_target_pairs={{0,2},{2,0},{4,6},{6,4},{8,10},{10,8},{12,14},{14,12},{16,18},{18,... | collective-permute-start | bytes 50331656 | tf_op jit(solution)/shard_map/cond/branch_1_fun/ppermute | solution.py:527
  200.2 364.1 %collective-permute-start.2 = (f32[2048,2048]{1,0:T(8,128)}, f32[2048,2048]{1,0:T(8,128)}, u32[]{:S(2)}, u32[]{:S(2)}) collective-permute-start(f32[2048,2048]{1,0:T(8,128)} %add.36), channel_id=1, source_target_pairs={{0,4},{2,6},{4,0},{6,2},{8,12},{10,14},{12,8},{14,10},{16,20},{18,... | collective-permute-start | bytes 50331656 | tf_op jit(solution)/shard_map/cond/branch_1_fun/ppermute | solution.py:527
  576.0 361.6 %collective-permute-start.3 = (f32[2048,2048]{1,0:T(8,128)S(1)}, f32[2048,2048]{1,0:T(8,128)}, u32[]{:S(2)}, u32[]{:S(2)}) collective-permute-start(f32[2048,2048]{1,0:T(8,128)S(1)} %add.37), channel_id=1, source_target_pairs={{0,8},{2,10},{4,12},{6,14},{8,0},{10,2},{12,4},{14,6},{16,24},{18,... | collective-permute-start | bytes 50331656 | tf_op jit(solution)/shard_map/cond/branch_1_fun/ppermute | solution.py:527
  949.7 362.3 %collective-permute-start.4 = (f32[2048,2048]{1,0:T(8,128)}, f32[2048,2048]{1,0:T(8,128)}, u32[]{:S(2)}, u32[]{:S(2)}) collective-permute-start(f32[2048,2048]{1,0:T(8,128)} %add.38), channel_id=1, source_target_pairs={{0,16},{2,18},{4,20},{6,22},{8,24},{10,26},{12,28},{14,30},{16,0},... | collective-permute-start | bytes 50331656 | tf_op jit(solution)/shard_map/cond/branch_1_fun/ppermute | solution.py:527
  1323.7 359.8 %collective-permute-start.5 = (f32[2048,2048]{1,0:T(8,128)S(1)}, f32[2048,2048]{1,0:T(8,128)}, u32[]{:S(2)}, u32[]{:S(2)}) collective-permute-start(f32[2048,2048]{1,0:T(8,128)S(1)} %add.39), channel_id=1, source_target_pairs={{0,32},{2,34},{4,36},{6,38},{8,40},{10,42},{12,44},{14,46},{16,48}... | collective-permute-start | bytes 50331656 | tf_op jit(solution)/shard_map/cond/branch_1_fun/ppermute | solution.py:527
  1695.6 360.4 %collective-permute-start.6 = (f32[2048,2048]{1,0:T(8,128)}, f32[2048,2048]{1,0:T(8,128)S(1)}, u32[]{:S(2)}, u32[]{:S(2)}) collective-permute-start(f32[2048,2048]{1,0:T(8,128)} %add.40), channel_id=1, source_target_pairs={{0,64},{2,66},{4,68},{6,70},{8,72},{10,74},{12,76},{14,78},{16,80}... | collective-permute-start | bytes 50331656 | tf_op jit(solution)/shard_map/cond/branch_1_fun/ppermute | solution.py:527
  2438.6 43.3 %collective-permute-start.7 = (f32[256,2048]{1,0:T(8,128)S(1)}, f32[256,2048]{1,0:T(8,128)}, u32[]{:S(2)}, u32[]{:S(2)}) collective-permute-start(f32[256,2048]{1,0:T(8,128)S(1)} %fusion.6), channel_id=1, source_target_pairs={{0,1},{1,0},{2,3},{3,2},{4,5},{5,4},{6,7},{7,6},{8,9},{9,8},{10,11... | collective-permute-start | bytes 6291464 | tf_op jit(solution)/shard_map/cond/branch_1_fun/ppermute | solution.py:518
  2500.1 20.0 collective-permute-start.8

commit v6 on v5

--- a/solution.py
+++ b/solution.py
@@ -37,7 +37,7 @@
     )
 
 SEGMENTS = ((0, 4), (8, 4), (16, 4), (24, 4), (32, 2))
-EARLY = 2
+EARLY = 3
 
 
 def inverse_factor(s_ref, m_ref, bad_ref):

time: 2530 us -> 2530 us (level)
  no operation moved by 1% of the time
where the time goes in v6:
time: 2530 us
  waiting for transfers between devices  1900 us (75%)
  Pallas kernels  493 us (19%)
  other arithmetic  74.4 us (3%)
  matrix products  39.7 us (2%)
    ppermute x6, waiting for transfers between devices, direct_step(): cov = cov + lax.ppermute(cov, 'rows', [(r, r ^ hop) for r in range(ranks)])  1820 us
    pallas_call x1, Pallas kernels, direct_step(): pl.pallas_call(direct_kernel, out_shape=jax.ShapeDtypeStruct((n, n), jnp....  358 us
    pallas_call x1, Pallas kernels, whole_step(): pl.pallas_call(functools.partial(step_kernel, total, ridge_weight), out_s...  135 us
    ppermute x3, waiting for transfers between devices, swapped(): return lax.ppermute(x, 'blk', [(0, 1), (1, 0)])  75.1 us
    add x5, other arithmetic, direct_step(): cov = cov + lax.ppermute(cov, 'rows', [(r, r ^ hop) for r in range(ranks)])  59.9 us
  transfers between devices with their start and end apart: 9, of which 9 were waited for; matrix products, arithmetic and copies ran while one was open for 0% of the time, Pallas kernels for 0%

profile of v6, /device:TPU:0, one launch (start us, length us, event | category | flops | bytes accessed | tf_op | source)
XLA Modules:
  0.0 2525.9 jit_solution(11429661063231917241)
XLA Ops:
  0.6 0.0 copy-start.1
  0.6 135.1 %shard_map.63 = (f32[128,2048]{1,0:T(8,128)S(1)}, f32[128,2048]{1,0:T(8,128)}, f32[1]{0:T(128)}) custom-call(bf16[256,4096]{1,0:T(8,128)(2,1)} %text_emb.1, bf16[256,4096]{1,0:T(8,128)(2,1)} %quant_emb.1, bf16[4096,1024]{1,0:T(8,128)(2,1)} %text_head.1, bf16[4096,1024]{1,0:T(8,128)(2,1)} %quant_head.1), custom_call_target="tpu_custom_call" | custom-call | tf_op jit(solution)/shard_map/pallas_call | solution.py:388
  136.5 0.0 copy-done.1
  136.5 2388.2 %conditional.1 = (f32[128,2048]{1,0:T(8,128)}, f32[128,2048]{1,0:T(8,128)}) conditional(s32[]{:T(128)} %bitcast.5, (f32[1]{0:T(128)}, f32[128,2048]{1,0:T(8,128)S(1)}, f32[128,2048]{1,0:T(8,128)}) %tuple.15, (bf16[256,4096]{1,0:T(8,128)(2,1)S(1)}, bf16[4096,1024]{1,0:T(8,128)(2,1)}, bf16[256,4096]{1,0:T(8,128)(2,1)}, ...), branch_computations={%region_0.0_spmd, %region_1.2_spmd} | conditional | flops 32265207808 | bytes 850395520 | solution.py:553
  136.5 0.0 copy-start
  136.5 0.0 copy-start.2
  136.5 5.9 fusion
  142.4 0.0 copy-done
  142.4 0.5 copy-done.2
  142.9 2.4 fusion.1
  145.3 0.4 fusion.5
  145.7 1.1 collective-permute-start
  146.7 12.2 collective-permute-done
  158.9 2.4 fusion.7
  161.4 0.1 collective-permute-start.1
  161.5 25.3 %collective-permute-done.1 = f32[2048,2048]{1,0:T(8,128)} collective-permute-done((f32[2048,2048]{1,0:T(8,128)S(1)}, f32[2048,2048]{1,0:T(8,128)}, u32[]{:S(2)}, u32[]{:S(2)}) %collective-permute-start.1) | collective-permute-done | bytes 16777248 | tf_op jit(solution)/shard_map/cond/branch_1_fun/ppermute | solution.py:527
  186.7 12.3 add.36
  199.1 3.1 collective-permute-start.2
  202.2 361.0 %collective-permute-done.2 = f32[2048,2048]{1,0:T(8,128)} collective-permute-done((f32[2048,2048]{1,0:T(8,128)}, f32[2048,2048]{1,0:T(8,128)}, u32[]{:S(2)}, u32[]{:S(2)}) %collective-permute-start.2) | collective-permute-done | bytes 16777248 | tf_op jit(solution)/shard_map/cond/branch_1_fun/ppermute | solution.py:527
  563.1 11.6 add.37
  574.8 0.9 collective-permute-start.3
  575.6 360.8 %collective-permute-done.3 = f32[2048,2048]{1,0:T(8,128)} collective-permute-done((f32[2048,2048]{1,0:T(8,128)S(1)}, f32[2048,2048]{1,0:T(8,128)}, u32[]{:S(2)}, u32[]{:S(2)}) %collective-permute-start.3) | collective-permute-done | bytes 16777248 | tf_op jit(solution)/shard_map/cond/branch_1_fun/ppermute | solution.py:527
  936.4 12.1 add.38
  948.5 2.2 collective-permute-start.4
  950.8 360.1 %collective-permute-done.4 = f32[2048,2048]{1,0:T(8,128)} collective-permute-done((f32[2048,2048]{1,0:T(8,128)}, f32[2048,2048]{1,0:T(8,128)}, u32[]{:S(2)}, u32[]{:S(2)}) %collective-permute-start.4) | collective-permute-done | bytes 16777248 | tf_op jit(solution)/shard_map/cond/branch_1_fun/ppermute | solution.py:527
  1310.9 11.6 add.39
  1322.5 1.9 collective-permute-start.5
  1324.4 358.3 %collective-permute-done.5 = f32[2048,2048]{1,0:T(8,128)} collective-permute-done((f32[2048,2048]{1,0:T(8,128)S(1)}, f32[2048,2048]{1,0:T(8,128)}, u32[]{:S(2)}, u32[]{:S(2)}) %collective-permute-start.5) | collective-permute-done | bytes 16777248 | tf_op jit(solution)/shard_map/cond/branch_1_fun/ppermute | solution.py:527
  1682.7 12.1 add.40
  1694.8 4.3 collective-permute-start.6
  1699.1 357.8 %collective-permute-done.6 = f32[2048,2048]{1,0:T(8,128)S(1)} collective-permute-done((f32[2048,2048]{1,0:T(8,128)}, f32[2048,2048]{1,0:T(8,128)S(1)}, u32[]{:S(2)}, u32[]{:S(2)}) %collective-permute-start.6) | collective-permute-done | bytes 16777248 | tf_op jit(solution)/shard_map/cond/branch_1_fun/ppermute | solution.py:527
  2056.9 12.6 select_add_fusion.c_ref
  2069.5 358.1 %branch_1_fun.1 = f32[2048,2048]{1,0:T(8,128)} custom-call(f32[2048,2048]{1,0:T(8,128)} %select_add_fusion.c_ref), custom_call_target="tpu_custom_call" | custom-call | tf_op jit(solution)/shard_map/cond/branch_1_fun/pallas_call | solution.py:530
  2427.5 12.0 fusion.6
  2439.5 1.2 collective-permute-start.7
  2440.8 43.1 %collective-permute-done.7 = f32[256,2048]{1,0:T(8,128)} collective-permute-done((f32[256,2048]{1,0:T(8,128)S(1)}, f32[256,2048]{1,0:T(8,128)}, u32[]{:S(2)}, u32[]{:S(2)}) %collective-permute-start.7) | collective-permute-done | bytes 2097184 | tf_op jit(solution)/shard_map/cond/branch_1_fun/ppermute | solution.py:518
  2483.8 17.1 fusion.10
  2500.9 1.1 constant_dynamic-slice_fusion
  2502.0 1.1 collective-permute-start.8
  2503.1 19.8 collective-permute-done.8
  2522.9 1.5 dynamic-slice_select_fusion
Async XLA Ops:
  0.6 135.8 %copy-start.1 = (bf16[256,4096]{1,0:T(8,128)(2,1)S(1)}, bf16[256,4096]{1,0:T(8,128)(2,1)}, u32[]{:S(2)}) copy-start(bf16[256,4096]{1,0:T(8,128)(2,1)} %text_emb.1) | copy-start | bytes 6291460
  136.5 5.9 copy-start
  136.5 6.4 copy-start.2
  145.7 13.3 collective-permute-start
  161.4 25.4 %collective-permute-start.1 = (f32[2048,2048]{1,0:T(8,128)S(1)}, f32[2048,2048]{1,0:T(8,128)}, u32[]{:S(2)}, u32[]{:S(2)}) collective-permute-start(f32[2048,2048]{1,0:T(8,128)S(1)} %fusion.7), channel_id=1, source_target_pairs={{0,2},{2,0},{4,6},{6,4},{8,10},{10,8},{12,14},{14,12},{16,18},{18,... | collective-permute-start | bytes 50331656 | tf_op jit(solution)/shard_map/cond/branch_1_fun/ppermute | solution.py:527
  199.1 364.1 %collective-permute-start.2 = (f32[2048,2048]{1,0:T(8,128)}, f32[2048,2048]{1,0:T(8,128)}, u32[]{:S(2)}, u32[]{:S(2)}) collective-permute-start(f32[2048,2048]{1,0:T(8,128)} %add.36), channel_id=1, source_target_pairs={{0,4},{2,6},{4,0},{6,2},{8,12},{10,14},{12,8},{14,10},{16,20},{18,... | collective-permute-start | bytes 50331656 | tf_op jit(solution)/shard_map/cond/branch_1_fun/ppermute | solution.py:527
  574.8 361.6 %collective-permute-start.3 = (f32[2048,2048]{1,0:T(8,128)S(1)}, f32[2048,2048]{1,0:T(8,128)}, u32[]{:S(2)}, u32[]{:S(2)}) collective-permute-start(f32[2048,2048]{1,0:T(8,128)S(1)} %add.37), channel_id=1, source_target_pairs={{0,8},{2,10},{4,12},{6,14},{8,0},{10,2},{12,4},{14,6},{16,24},{18,... | collective-permute-start | bytes 50331656 | tf_op jit(solution)/shard_map/cond/branch_1_fun/ppermute | solution.py:527
  948.5 362.3 %collective-permute-start.4 = (f32[2048,2048]{1,0:T(8,128)}, f32[2048,2048]{1,0:T(8,128)}, u32[]{:S(2)}, u32[]{:S(2)}) collective-permute-start(f32[2048,2048]{1,0:T(8,128)} %add.38), channel_id=1, source_target_pairs={{0,16},{2,18},{4,20},{6,22},{8,24},{10,26},{12,28},{14,30},{16,0},... | collective-permute-start | bytes 50331656 | tf_op jit(solution)/shard_map/cond/branch_1_fun/ppermute | solution.py:527
  1322.5 360.2 %collective-permute-start.5 = (f32[2048,2048]{1,0:T(8,128)S(1)}, f32[2048,2048]{1,0:T(8,128)}, u32[]{:S(2)}, u32[]{:S(2)}) collective-permute-start(f32[2048,2048]{1,0:T(8,128)S(1)} %add.39), channel_id=1, source_target_pairs={{0,32},{2,34},{4,36},{6,38},{8,40},{10,42},{12,44},{14,46},{16,48}... | collective-permute-start | bytes 50331656 | tf_op jit(solution)/shard_map/cond/branch_1_fun/ppermute | solution.py:527
  1694.8 362.1 %collective-permute-start.6 = (f32[2048,2048]{1,0:T(8,128)}, f32[2048,2048]{1,0:T(8,128)S(1)}, u32[]{:S(2)}, u32[]{:S(2)}) collective-permute-start(f32[2048,2048]{1,0:T(8,128)} %add.40), channel_id=1, source_target_pairs={{0,64},{2,66},{4,68},{6,70},{8,72},{10,74},{12,76},{14,78},{16,80}... | collective-permute-start | bytes 50331656 | tf_op jit(solution)/shard_map/cond/branch_1_fun/ppermute | solution.py:527
  2439.5 44.3 %collective-permute-start.7 = (f32[256,2048]{1,0:T(8,128)S(1)}, f32[256,2048]{1,0:T(8,128)}, u32[]{:S(2)}, u32[]{:S(2)}) collective-permute-start(f32[256,2048]{1,0:T(8,128)S(1)} %fusion.6), channel_id=1, source_target_pairs={{0,1},{1,0},{2,3},{3,2},{4,5},{5,4},{6,7},{7,6},{8,9},{9,8},{10,11... | collective-permute-start | bytes 6291464 | tf_op jit(solution)/shard_map/cond/branch_1_fun/ppermute | solution.py:518
  2502.0 20.9 collective-permute-start.8
